TPU v7x, 32 devices: a whole 2x2x4 slice. The times are simulated.
32 devices in a mesh: sec: 8 (over y, x, core), op: 4 (over z).
Axes of the slice: x: 2, y: 2, z: 4, core: 2. Of those that a mesh axis runs over, the one named last changes fastest.
Arguments:
- environment: float32 [8, 56, 256, 256], P('sec', 'op'), may hold values from -6 to 6
- mps: float32 [8, 4, 256, 256], P('sec'), may hold values from -0.375 to 0.375
- mpo: float32 [56, 4, 56], P('op'), may hold values from -0.75 to 0.75
- mpo_pattern: int32 [56, 4], P('op'), may hold values 0 or 1
- state_shift: int32 [4], replicated, may hold values from 0 to 7, as said below
- sector_dims: int32 [8], replicated, may hold values from 1 to 256, 1024 in all
Outputs:
- new_environment: float32 [8, 56, 4, 256], P('sec', 'op')
Inputs may be any that keep to these rules, and one draw needn't show every extreme that they name: `state_shift`: the four shifts are 0, 1, 4 and 7, assigned to the physical states in an order drawn from the seed. `sector_dims`: the live states sum to 1024.
All inputs are finite; a program needn't handle non-finite values. No bound on the sum of `mpo_pattern` on one device may be relied on, other than what follows from the above.
Results may differ from a plain program's by a relative error of at most 0.000088.
Values sent between devices are 32-bit elements; how exact they have to be, the bound alone decides.
No kernel may reach another device: no remote copies, remote signals or barrier semaphores. Data moves between devices by JAX's collectives and lax.ppermute only.
A program may use at most 64 MiB of HBM per device.

v0:
```python
import jax
import jax.numpy as jnp
from jax import lax
from jax.sharding import PartitionSpec as P

ROWS = 4


def passed_along(value, axis, steps):
    count = lax.axis_size(axis)
    pairs = [(source, (source + steps) % count) for source in range(count)]
    return lax.ppermute(value, axis, pairs)


def local(environment, mps, mpo, mpo_pattern, state_shift, sector_dims):
    highest = lax.Precision.HIGHEST
    sectors = lax.axis_size("sec")
    here = lax.axis_index("sec")
    width = mps.shape[-1]
    positions = jnp.arange(width, dtype=jnp.int32)
    labels = jnp.arange(sectors, dtype=jnp.int32)
    target = (here + state_shift) % sectors
    dims_out = jnp.sum(
        jnp.where(target[:, None] == labels[None, :], sector_dims[None, :], 0), axis=1
    )
    dims_in = jnp.sum(jnp.where(labels == here, sector_dims, 0))
    live_in = (positions < dims_in).astype(jnp.float32)
    live_out = (positions[None, :] < dims_out[:, None]).astype(jnp.float32)
    masked = mps[0] * live_in[None, :, None] * live_out[:, None, :]
    left = masked[:, :, :ROWS]
    half = jnp.einsum("sar,wab->swrb", left, environment[0], precision=highest)
    blocks = jnp.einsum("swrb,sbc->swrc", half, masked, precision=highest)
    remain = state_shift % sectors
    routed = blocks
    for level in range((sectors - 1).bit_length()):
        moving = (remain // (1 << level) % 2 == 1)[:, None, None, None]
        outgoing = jnp.where(moving, routed, 0.0)
        arriving = passed_along(outgoing, "sec", 1 << level)
        routed = jnp.where(moving, arriving, routed)
    coef = mpo * mpo_pattern[:, :, None].astype(jnp.float32)
    summed = lax.psum_scatter(
        jnp.einsum("swrc,wsv->vrc", routed, coef, precision=highest),
        "op",
        scatter_dimension=0,
        tiled=True,
    )
    return summed[None]


def solution(mesh):
    in_specs = (
        P("sec", "op", None, None),
        P("sec", None, None, None),
        P("op", None, None),
        P("op", None),
        P(),
        P(),
    )
    out_specs = P("sec", "op", None, None)
    return jax.shard_map(local, mesh=mesh, in_specs=in_specs, out_specs=out_specs, check_vma=False)
```

profile of v0, /device:TPU:0, one launch (start us, length us, event | category | flops | bytes accessed | tf_op | source)
XLA Modules:
  0.0 84.9 jit_solution(15415171174693530631)
XLA Ops:
  6.5 0.0 all-reduce.3.cloned.1.call-start
  6.5 0.7 fusion.15
  7.2 1.6 %copy.16 = f32[1,4,256,256]{2,3,1,0:T(8,128)S(1)} copy(f32[1,4,256,256]{3,2,1,0:T(8,128)} %param.7) | data formatting | bytes 2097152 | tf_op args[1]
  8.8 0.7 and_select_fusion
  9.5 1.3 %fusion.17 = s32[]{:T(128)} fusion(s32[8]{0:T(128)} %param.11, s32[]{:T(128)S(6)} %axis_index.15), kind=kLoop, calls=%fused_computation.50 | loop fusion | flops 23 | bytes 40 | tf_op jit(solution)/shard_map/reduce_sum | solution.py:26
  10.8 0.8 select_reduce_fusion
  11.6 0.1 fusion.13
  11.7 0.6 compare_convert_fusion
  12.3 0.2 fusion.7
  12.5 0.0 copy-start.1
  12.6 0.0 copy-start
  12.6 3.9 %fusion.2 = f32[4,14,4,256]{3,2,1,0:T(4,128)S(1)} fusion(f32[1,14,256,256]{3,2,1,0:T(8,128)} %param.6, f32[4,256,256]{1,2,0:T(8,128)S(1)} %fusion.7), kind=kOutput, calls=%fused_computation.3 | convolution fusion | flops 176160768 | bytes 3915776 | tf_op jit(solution)/shard_map/sar,wab->swrb/dot_general | solution.py:31
  16.5 0.0 copy-start.2
  16.5 1.1 %broadcast_select_fusion.2 = (f32[4,14,4,256]{3,1,2,0:T(8,128)S(1)}, f32[4,14,4,256]{3,1,2,0:T(8,128)S(1)}) fusion(pred[4]{0:T(512)(128)(4,1)S(1)} %get-tuple-element.9, f32[4,256,256]{1,2,0:T(8,128)S(1)} %fusion.7, f32[4,14,4,256]{3,2,1,0:T(4,128)S(1)} %fusion.2), kind=kOutput, calls=%fused_computation.12 | convolution fusion | flops 176218112 | bytes 1736708 | tf_op jit(solution)/shard_map/swrb,sbc->swrc/dot_general | solution.py:32
  17.6 0.5 collective-permute-start
  18.1 6.9 %collective-permute-done = f32[4,14,4,256]{3,1,2,0:T(8,128)S(1)} collective-permute-done((f32[4,14,4,256]{3,1,2,0:T(8,128)S(1)}, f32[4,14,4,256]{3,1,2,0:T(8,128)S(1)}, u32[]{:S(2)}, u32[]{:S(2)}) %collective-permute-start) | collective-permute-done | bytes 229408 | tf_op jit(solution)/shard_map/ppermute | solution.py:12
  25.0 0.1 broadcast_select_fusion.1
  25.2 1.4 %collective-permute-start.1 = (f32[4,14,4,256]{3,1,2,0:T(8,128)S(1)}, f32[4,14,4,256]{3,1,2,0:T(8,128)S(1)}, u32[]{:S(2)}, u32[]{:S(2)}) collective-permute-start(f32[4,14,4,256]{3,1,2,0:T(8,128)S(1)} %get-tuple-element.5), channel_id=1, source_target_pairs={{0,8},{4,12},{8,16},{12,20},{16,24},{20,28},{24,0},{28,4},{1,9},{5... | collective-permute-start | bytes 688136 | tf_op jit(solution)/shard_map/ppermute | solution.py:12
  26.6 6.7 %collective-permute-done.1 = f32[4,14,4,256]{3,1,2,0:T(8,128)S(1)} collective-permute-done((f32[4,14,4,256]{3,1,2,0:T(8,128)S(1)}, f32[4,14,4,256]{3,1,2,0:T(8,128)S(1)}, u32[]{:S(2)}, u32[]{:S(2)}) %collective-permute-start.1) | collective-permute-done | bytes 229408 | tf_op jit(solution)/shard_map/ppermute | solution.py:12
  33.3 0.1 broadcast_select_fusion
  33.4 1.6 %collective-permute-start.2 = (f32[4,14,4,256]{3,1,2,0:T(8,128)S(1)}, f32[4,14,4,256]{3,1,2,0:T(8,128)S(1)}, u32[]{:S(2)}, u32[]{:S(2)}) collective-permute-start(f32[4,14,4,256]{3,1,2,0:T(8,128)S(1)} %broadcast_select_fusion), channel_id=1, source_target_pairs={{0,16},{4,20},{8,24},{12,28},{16,0},{20,4},{24,8},{28,12},{1,17},{... | collective-permute-start | bytes 688136 | tf_op jit(solution)/shard_map/ppermute | solution.py:12
  35.0 0.0 copy-done.1
  35.0 0.1 copy.15
  35.1 0.0 copy-done
  35.1 0.1 broadcast_multiply_fusion
  35.2 4.6 %collective-permute-done.2 = f32[4,14,4,256]{3,1,2,0:T(8,128)S(1)} collective-permute-done((f32[4,14,4,256]{3,1,2,0:T(8,128)S(1)}, f32[4,14,4,256]{3,1,2,0:T(8,128)S(1)}, u32[]{:S(2)}, u32[]{:S(2)}) %collective-permute-start.2) | collective-permute-done | bytes 229408 | tf_op jit(solution)/shard_map/ppermute | solution.py:12
  39.8 0.4 convolution_bitcast_fusion
  40.3 0.8 copy.21
  41.1 0.0 all-reduce.3.cloned.1.call-update
  41.1 0.0 copy-done.2
  41.1 0.6 dynamic-slice
  42.3 34.3 %all-reduce.3.cloned.1.call-done = f32[56,4,256]{2,1,0:T(4,128)} async-done(((f32[56,4,256]{2,1,0:T(4,128)}), f32[56,4,256]{2,1,0:T(4,128)}) %all-reduce.3.cloned.1.call-update) | async-done | bytes 229392
  76.6 1.4 %dynamic-slice_bitcast_fusion = f32[1,14,4,256]{3,2,1,0:T(4,128)} fusion(f32[56,4,256]{2,1,0:T(4,128)} %all-reduce.3.cloned.1.call-done, u32[]{:T(128)S(6)} %multiply.1), kind=kLoop, calls=%fused_computation.16 | loop fusion | bytes 114692 | tf_op jit(solution)/shard_map/broadcast_in_dim | solution.py:47
  (2 shorter events, 0.0 us)
Async XLA Ops:
  6.5 70.1 %all-reduce.3.cloned.1.call-start = ((), (), s32[]{:S(2)}) async-start(), calls=%async_computation | async-start | bytes 458752
  12.5 22.5 %copy-start.1 = (s32[14,4]{0,1:T(4,128)S(1)}, s32[14,4]{0,1:T(4,128)}, u32[]{:S(2)}) copy-start(s32[14,4]{0,1:T(4,128)} %param.9) | copy-start | bytes 676
  12.6 22.6 %copy-start = (f32[14,4,56]{2,1,0:T(4,128)S(1)}, f32[14,4,56]{2,1,0:T(4,128)}, u32[]{:S(2)}) copy-start(f32[14,4,56]{2,1,0:T(4,128)} %param.8) | copy-start | bytes 37636
  16.5 24.6 %copy-start.2 = (u32[32]{0:T(128)S(1)}, u32[32]{0:T(128)}, u32[]{:S(2)}) copy-start(u32[32]{0:T(128)} %constant.87) | copy-start | bytes 388
  17.6 7.4 %collective-permute-start = (f32[4,14,4,256]{3,1,2,0:T(8,128)S(1)}, f32[4,14,4,256]{3,1,2,0:T(8,128)S(1)}, u32[]{:S(2)}, u32[]{:S(2)}) collective-permute-start(f32[4,14,4,256]{3,1,2,0:T(8,128)S(1)} %get-tuple-element.11), channel_id=1, source_target_pairs={{0,4},{4,8},{8,12},{12,16},{16,20},{20,24},{24,28},{28,0},{1,5},{5... | collective-permute-start | bytes 688136 | tf_op jit(solution)/shard_map/ppermute | solution.py:12
  25.2 8.1 %collective-permute-start.1 = (f32[4,14,4,256]{3,1,2,0:T(8,128)S(1)}, f32[4,14,4,256]{3,1,2,0:T(8,128)S(1)}, u32[]{:S(2)}, u32[]{:S(2)}) collective-permute-start(f32[4,14,4,256]{3,1,2,0:T(8,128)S(1)} %get-tuple-element.5), channel_id=1, source_target_pairs={{0,8},{4,12},{8,16},{12,20},{16,24},{20,28},{24,0},{28,4},{1,9},{5... | collective-permute-start | bytes 688136 | tf_op jit(solution)/shard_map/ppermute | solution.py:12
  33.4 6.4 %collective-permute-start.2 = (f32[4,14,4,256]{3,1,2,0:T(8,128)S(1)}, f32[4,14,4,256]{3,1,2,0:T(8,128)S(1)}, u32[]{:S(2)}, u32[]{:S(2)}) collective-permute-start(f32[4,14,4,256]{3,1,2,0:T(8,128)S(1)} %broadcast_select_fusion), channel_id=1, source_target_pairs={{0,16},{4,20},{8,24},{12,28},{16,0},{20,4},{24,8},{28,12},{1,17},{... | collective-permute-start | bytes 688136 | tf_op jit(solution)/shard_map/ppermute | solution.py:12
Sparse Core Ops, SparseCore 0:
  41.2 35.3 all-reduce.2
where the time goes:
time: 85.2 us; the launch traced here: 84.9 us
  waiting for transfers between devices  52.6 us (62%)
  between operations  14.1 us (17%)
  matrix products  5.45 us (6%)
  other arithmetic  4.71 us (6%)
  local copies, waits for them, and re-layouts  4.48 us (5%)
  starting transfers between devices  3.51 us (4%)
    unnamed x2, waiting for transfers between devices  34.3 us
    ppermute x3, waiting for transfers between devices, passed_along(): return lax.ppermute(value, axis, pairs)  18.3 us
    dot_general x1, matrix products, local(): half = jnp.einsum('sar,wab->swrb', left, environment[0], precision=highest)  3.92 us
    ppermute x3, starting transfers between devices, passed_along(): return lax.ppermute(value, axis, pairs)  3.51 us
    unnamed x8, local copies, waits for them, and re-layouts  2.16 us
  transfers between devices with their start and end apart: 4, of which 4 were waited for; matrix products, arithmetic and copies ran while one was open for 1% of the time, Pallas kernels for 0%

commit v1 on v0

--- a/solution.py
+++ b/solution.py
@@ -4,9 +4,10 @@
 from jax.sharding import PartitionSpec as P
 
 ROWS = 4
+EXCHANGE = "permute"
 
 
-def passed_along(value, axis, steps):
+def shifted(value, axis, steps):
     count = lax.axis_size(axis)
     pairs = [(source, (source + steps) % count) for source in range(count)]
     return lax.ppermute(value, axis, pairs)
@@ -16,7 +17,10 @@
     highest = lax.Precision.HIGHEST
     sectors = lax.axis_size("sec")
     here = lax.axis_index("sec")
+    parts = lax.axis_size("op")
+    me = lax.axis_index("op")
     width = mps.shape[-1]
+    states = mps.shape[1]
     positions = jnp.arange(width, dtype=jnp.int32)
     labels = jnp.arange(sectors, dtype=jnp.int32)
     target = (here + state_shift) % sectors
@@ -30,21 +34,26 @@
     left = masked[:, :, :ROWS]
     half = jnp.einsum("sar,wab->swrb", left, environment[0], precision=highest)
     blocks = jnp.einsum("swrb,sbc->swrc", half, masked, precision=highest)
-    remain = state_shift % sectors
-    routed = blocks
-    for level in range((sectors - 1).bit_length()):
-        moving = (remain // (1 << level) % 2 == 1)[:, None, None, None]
-        outgoing = jnp.where(moving, routed, 0.0)
-        arriving = passed_along(outgoing, "sec", 1 << level)
-        routed = jnp.where(moving, arriving, routed)
+    steps = (0, 1, sectors // 2, sectors - 1)
+    ids = jnp.arange(states, dtype=jnp.int32)
+    picks = [jnp.sum(jnp.where(state_shift % sectors == step, ids, 0)) for step in steps]
+    routed = []
+    for step, pick in zip(steps, picks):
+        block = lax.dynamic_index_in_dim(blocks, pick, 0, keepdims=False)
+        routed.append(block if step == 0 else shifted(block, "sec", step))
     coef = mpo * mpo_pattern[:, :, None].astype(jnp.float32)
-    summed = lax.psum_scatter(
-        jnp.einsum("swrc,wsv->vrc", routed, coef, precision=highest),
-        "op",
-        scatter_dimension=0,
-        tiled=True,
-    )
-    return summed[None]
+    chosen = jnp.stack([lax.dynamic_index_in_dim(coef, pick, 1, keepdims=False) for pick in picks])
+    partial = jnp.einsum("kwrc,kwv->vrc", jnp.stack(routed), chosen, precision=highest)
+    chunk = partial.shape[0] // parts
+    pieces = partial.reshape((parts, chunk) + partial.shape[1:])
+    if EXCHANGE == "permute":
+        total = lax.dynamic_index_in_dim(pieces, me, 0, keepdims=False)
+        for step in range(1, parts):
+            send = lax.dynamic_index_in_dim(pieces, (me + step) % parts, 0, keepdims=False)
+            total = total + shifted(send, "op", step)
+    else:
+        total = jnp.sum(lax.all_to_all(pieces, "op", 0, 0, tiled=True), axis=0)
+    return total[None]
 
 
 def solution(mesh):

time: 85.2 us -> 38.3 us (0.45)
  waiting for transfers between devices: 52.6 us -> 9.26 us
  between operations: 14.1 us -> 7.71 us
  starting transfers between devices: 3.51 us -> 8.56 us
  local copies, waits for them, and re-layouts: 4.48 us -> 1.85 us
    unnamed x2 -> x0, waiting for transfers between devices: 34.3 us -> none
    ppermute x3 -> x6, waiting for transfers between devices: 18.3 us -> 9.26 us  [shifted(): return lax.ppermute(value, axis, pairs)]
    ppermute x3 -> x6, starting transfers between devices: 3.51 us -> 8.56 us  [shifted(): return lax.ppermute(value, axis, pairs)]
    broadcast_in_dim x1 -> x0, local copies, waits for them, and re-layouts: 1.44 us -> none  [local(): return summed[None]]
    unnamed x8 -> x5, local copies, waits for them, and re-layouts: 2.16 us -> 1.57 us
  transfers between devices with their start and end apart: 4 -> 6, of which waited for: 4 -> 6; matrix products, arithmetic and copies ran while one was open for 1% -> 1% of each run, Pallas kernels for 0% -> 0%
where the time goes in v1:
time: 38.3 us; the launch traced here: 38 us
  waiting for transfers between devices  9.26 us (24%)
  starting transfers between devices  8.56 us (22%)
  between operations  7.71 us (20%)
  matrix products  5.42 us (14%)
  other arithmetic  5.19 us (14%)
  local copies, waits for them, and re-layouts  1.85 us (5%)
    ppermute x6, waiting for transfers between devices, shifted(): return lax.ppermute(value, axis, pairs)  9.26 us
    ppermute x6, starting transfers between devices, shifted(): return lax.ppermute(value, axis, pairs)  8.56 us
    dot_general x1, matrix products, local(): half = jnp.einsum('sar,wab->swrb', left, environment[0], precision=highest)  3.91 us
    unnamed x5, local copies, waits for them, and re-layouts  1.57 us
    reduce_sum x1, other arithmetic, local(): dims_in = jnp.sum(jnp.where(labels == here, sector_dims, 0))  1.29 us
    dot_general x1, matrix products, local(): blocks = jnp.einsum('swrb,sbc->swrc', half, masked, precision=highest)  1.11 us
    reduce_sum x1, other arithmetic, local(): jnp.sum(jnp.where(target[:, None] == labels[None, :], sector_dims[None, :...  0.84 us
  transfers between devices with their start and end apart: 6, of which 6 were waited for; matrix products, arithmetic and copies ran while one was open for 1% of the time, Pallas kernels for 0%

profile of v1, /device:TPU:0, one launch (start us, length us, event | category | flops | bytes accessed | tf_op | source)
XLA Modules:
  0.0 38.0 jit_solution(6884264686028046942)
XLA Ops:
  0.0 0.7 %and_select_fusion.1 = (s32[4]{0:T(128)S(1)}, s32[4]{0:T(128)S(1)}) fusion(s32[4]{0:T(128)} %param.10, s32[]{:T(128)S(6)} %axis_index.23), kind=kLoop, calls=%fused_computation.56 | loop fusion | flops 92 | bytes 52 | tf_op jit(solution)/shard_map/jit(remainder)/select_n | solution.py:39
  0.7 0.7 %fusion.28 = (s32[]{:T(128)}, s32[]{:T(128)}, s32[]{:T(128)}, s32[]{:T(128)}) fusion(s32[4]{0:T(128)S(1)} %get-tuple-element.20), kind=kLoop, calls=%fused_computation.57 | loop fusion | flops 44 | bytes 32 | tf_op jit(solution)/shard_map/reduce_sum | solution.py:39
  6.4 1.6 %copy.25 = f32[1,4,256,256]{2,3,1,0:T(8,128)S(1)} copy(f32[1,4,256,256]{3,2,1,0:T(8,128)} %param.7) | data formatting | bytes 2097152 | tf_op args[1]
  8.0 1.3 %fusion.32 = s32[]{:T(128)} fusion(s32[8]{0:T(128)} %param.11, s32[]{:T(128)S(6)} %axis_index.23), kind=kLoop, calls=%fused_computation.61 | loop fusion | flops 23 | bytes 40 | tf_op jit(solution)/shard_map/reduce_sum | solution.py:30
  9.3 0.8 %select_reduce_fusion = s32[4]{0:T(128)S(1)} fusion(s32[8]{0:T(128)} %param.11, s32[4]{0:T(128)S(1)} %get-tuple-element.21), kind=kLoop, calls=%fused_computation.47 | loop fusion | flops 92 | bytes 64 | tf_op jit(solution)/shard_map/reduce_sum | solution.py:27
  10.1 0.1 fusion.27
  10.2 0.6 %compare_convert_fusion = f32[256]{0:T(256)S(1)} fusion(s32[]{:T(128)} %fusion.32), kind=kLoop, calls=%fused_computation.50 | loop fusion | flops 512 | bytes 1028 | tf_op jit(solution)/shard_map/convert_element_type | solution.py:31
  10.9 0.0 copy-start.1
  10.9 0.0 copy-start
  10.9 0.2 fusion.7
  11.1 3.9 %fusion.2 = f32[4,14,4,256]{3,2,1,0:T(4,128)S(1)} fusion(f32[1,14,256,256]{3,2,1,0:T(8,128)} %param.6, f32[4,256,256]{1,2,0:T(8,128)S(1)} %fusion.7), kind=kOutput, calls=%fused_computation.3 | convolution fusion | flops 176160768 | bytes 3915776 | tf_op jit(solution)/shard_map/sar,wab->swrb/dot_general | solution.py:35
  15.0 1.1 %fusion.5 = f32[4,14,4,256]{3,1,2,0:T(8,128)S(1)} fusion(f32[4,256,256]{1,2,0:T(8,128)S(1)} %fusion.7, f32[4,14,4,256]{3,2,1,0:T(4,128)S(1)} %fusion.2), kind=kOutput, calls=%fused_computation.4 | convolution fusion | flops 176160768 | bytes 1507328 | tf_op jit(solution)/shard_map/swrb,sbc->swrc/dot_general | solution.py:36
  18.7 3.4 %collective-permute-start.2 = (f32[14,4,256]{2,0,1:T(8,128)S(1)}, f32[14,4,256]{2,0,1:T(8,128)S(1)}, u32[]{:S(2)}, u32[]{:S(2)}) collective-permute-start(f32[14,4,256]{2,0,1:T(8,128)S(1)} %get-tuple-element.10), channel_id=1, source_target_pairs={{0,28},{4,0},{8,4},{12,8},{16,12},{20,16},{24,20},{28,24},{1,29},{... | collective-permute-start | bytes 172040 | tf_op jit(solution)/shard_map/ppermute | solution.py:13
  22.1 0.5 %collective-permute-start.1 = (f32[14,4,256]{2,0,1:T(8,128)S(1)}, f32[14,4,256]{2,0,1:T(8,128)S(1)}, u32[]{:S(2)}, u32[]{:S(2)}) collective-permute-start(f32[14,4,256]{2,0,1:T(8,128)S(1)} %get-tuple-element.11), channel_id=1, source_target_pairs={{0,16},{4,20},{8,24},{12,28},{16,0},{20,4},{24,8},{28,12},{1,17},{... | collective-permute-start | bytes 172040 | tf_op jit(solution)/shard_map/ppermute | solution.py:13
  22.6 0.0 collective-permute-start
  22.6 0.0 copy-done.1
  22.6 0.1 copy.20
  22.7 0.0 copy-done
  22.7 0.1 broadcast_multiply_fusion
  22.9 1.1 %collective-permute-done.2 = f32[14,4,256]{2,0,1:T(8,128)S(1)} collective-permute-done((f32[14,4,256]{2,0,1:T(8,128)S(1)}, f32[14,4,256]{2,0,1:T(8,128)S(1)}, u32[]{:S(2)}, u32[]{:S(2)}) %collective-permute-start.2) | collective-permute-done | bytes 57376 | tf_op jit(solution)/shard_map/ppermute | solution.py:13
  24.0 2.4 %collective-permute-done.1 = f32[14,4,256]{2,0,1:T(8,128)S(1)} collective-permute-done((f32[14,4,256]{2,0,1:T(8,128)S(1)}, f32[14,4,256]{2,0,1:T(8,128)S(1)}, u32[]{:S(2)}, u32[]{:S(2)}) %collective-permute-start.1) | collective-permute-done | bytes 57376 | tf_op jit(solution)/shard_map/ppermute | solution.py:13
  26.3 0.8 %collective-permute-done = f32[14,4,256]{2,0,1:T(8,128)S(1)} collective-permute-done((f32[14,4,256]{2,0,1:T(8,128)S(1)}, f32[14,4,256]{2,0,1:T(8,128)S(1)}, u32[]{:S(2)}, u32[]{:S(2)}) %collective-permute-start) | collective-permute-done | bytes 57376 | tf_op jit(solution)/shard_map/ppermute | solution.py:13
  27.2 0.4 %convolution_bitcast_fusion = f32[56,4,256]{2,0,1:T(8,128)S(1)} fusion(f32[1,14,4,256]{3,1,2,0:T(8,128)S(1)} %bitcast.68, f32[1,14,4,256]{3,1,2,0:T(8,128)S(1)} %bitcast.69, f32[1,14,4,256]{3,1,2,0:T(8,128)S(1)} %bitcast.70, f32[1,14,4,256]{3,1,2,0:T(8,128)S(1)} %get-tuple-element.9, f32[1,14,56]{2,1,0:T(8,128)S(1)} %copy.24, f32[1,14,56]{2,1,0:T(8,128)S(1)} %copy.23, ...), kind=kOutput, calls=%fused_computation.2 | convolution fusion | flops 38716608 | bytes 471296 | tf_op jit(solution)/shard_map/kwrc,kwv->vrc/dot_general | solution.py:46
  27.6 0.1 copy.29
  27.7 3.7 %collective-permute-start.5 = (f32[14,4,256]{2,1,0:T(4,128)S(1)}, f32[14,4,256]{2,1,0:T(4,128)S(1)}, u32[]{:S(2)}, u32[]{:S(2)}) collective-permute-start(f32[14,4,256]{2,1,0:T(4,128)S(1)} %get-tuple-element.14), channel_id=1, source_target_pairs={{0,3},{1,0},{2,1},{3,2},{4,7},{5,4},{6,5},{7,6},{8,11},{9,8},{10,9... | collective-permute-start | bytes 172040 | tf_op jit(solution)/shard_map/ppermute | solution.py:13
  31.4 0.0 collective-permute-start.4
  31.4 1.0 %collective-permute-start.3 = (f32[14,4,256]{2,1,0:T(4,128)S(1)}, f32[14,4,256]{2,1,0:T(4,128)S(1)}, u32[]{:S(2)}, u32[]{:S(2)}) collective-permute-start(f32[14,4,256]{2,1,0:T(4,128)S(1)} %get-tuple-element.13), channel_id=1, source_target_pairs={{0,1},{1,2},{2,3},{3,0},{4,5},{5,6},{6,7},{7,4},{8,9},{9,10},{10,1... | collective-permute-start | bytes 172040 | tf_op jit(solution)/shard_map/ppermute | solution.py:13
  32.4 0.8 %collective-permute-done.5 = f32[14,4,256]{2,1,0:T(4,128)S(1)} collective-permute-done((f32[14,4,256]{2,1,0:T(4,128)S(1)}, f32[14,4,256]{2,1,0:T(4,128)S(1)}, u32[]{:S(2)}, u32[]{:S(2)}) %collective-permute-start.5) | collective-permute-done | bytes 57376 | tf_op jit(solution)/shard_map/ppermute | solution.py:13
  33.2 3.2 %collective-permute-done.4 = f32[14,4,256]{2,1,0:T(4,128)S(1)} collective-permute-done((f32[14,4,256]{2,1,0:T(4,128)S(1)}, f32[14,4,256]{2,1,0:T(4,128)S(1)}, u32[]{:S(2)}, u32[]{:S(2)}) %collective-permute-start.4) | collective-permute-done | bytes 57376 | tf_op jit(solution)/shard_map/ppermute | solution.py:13
  36.4 0.9 %collective-permute-done.3 = f32[14,4,256]{2,1,0:T(4,128)S(1)} collective-permute-done((f32[14,4,256]{2,1,0:T(4,128)S(1)}, f32[14,4,256]{2,1,0:T(4,128)S(1)}, u32[]{:S(2)}, u32[]{:S(2)}) %collective-permute-start.3) | collective-permute-done | bytes 57376 | tf_op jit(solution)/shard_map/ppermute | solution.py:13
  37.3 0.7 %fusion.18 = f32[1,14,4,256]{3,2,1,0:T(4,128)} fusion(f32[14,4,256]{2,1,0:T(4,128)S(1)} %collective-permute-done.5, f32[14,4,256]{2,1,0:T(4,128)S(1)} %collective-permute-done.4, f32[14,4,256]{2,1,0:T(4,128)S(1)} %collective-permute-done.3, f32[4,14,4,256]{3,2,1,0:T(4,128)S(1)} %bitcast.67, s32[]{:T(128)S(6)} %select_n.94), kind=kLoop, calls=%fused_computation.22 | loop fusion | flops 43008 | bytes 286724 | tf_op jit(solution)/shard_map/broadcast_in_dim | solution.py:56
  (8 shorter events, 0.1 us)
Async XLA Ops:
  10.9 11.7 %copy-start.1 = (s32[14,4]{0,1:T(4,128)S(1)}, s32[14,4]{0,1:T(4,128)}, u32[]{:S(2)}) copy-start(s32[14,4]{0,1:T(4,128)} %param.9) | copy-start | bytes 676
  10.9 11.8 %copy-start = (f32[14,4,56]{2,1,0:T(4,128)S(1)}, f32[14,4,56]{2,1,0:T(4,128)}, u32[]{:S(2)}) copy-start(f32[14,4,56]{2,1,0:T(4,128)} %param.8) | copy-start | bytes 37636
  18.7 5.3 %collective-permute-start.2 = (f32[14,4,256]{2,0,1:T(8,128)S(1)}, f32[14,4,256]{2,0,1:T(8,128)S(1)}, u32[]{:S(2)}, u32[]{:S(2)}) collective-permute-start(f32[14,4,256]{2,0,1:T(8,128)S(1)} %get-tuple-element.10), channel_id=1, source_target_pairs={{0,28},{4,0},{8,4},{12,8},{16,12},{20,16},{24,20},{28,24},{1,29},{... | collective-permute-start | bytes 172040 | tf_op jit(solution)/shard_map/ppermute | solution.py:13
  22.1 4.3 %collective-permute-start.1 = (f32[14,4,256]{2,0,1:T(8,128)S(1)}, f32[14,4,256]{2,0,1:T(8,128)S(1)}, u32[]{:S(2)}, u32[]{:S(2)}) collective-permute-start(f32[14,4,256]{2,0,1:T(8,128)S(1)} %get-tuple-element.11), channel_id=1, source_target_pairs={{0,16},{4,20},{8,24},{12,28},{16,0},{20,4},{24,8},{28,12},{1,17},{... | collective-permute-start | bytes 172040 | tf_op jit(solution)/shard_map/ppermute | solution.py:13
  22.6 4.6 %collective-permute-start = (f32[14,4,256]{2,0,1:T(8,128)S(1)}, f32[14,4,256]{2,0,1:T(8,128)S(1)}, u32[]{:S(2)}, u32[]{:S(2)}) collective-permute-start(f32[14,4,256]{2,0,1:T(8,128)S(1)} %get-tuple-element.12), channel_id=1, source_target_pairs={{0,4},{4,8},{8,12},{12,16},{16,20},{20,24},{24,28},{28,0},{1,5},{5... | collective-permute-start | bytes 172040 | tf_op jit(solution)/shard_map/ppermute | solution.py:13
  27.7 5.5 %collective-permute-start.5 = (f32[14,4,256]{2,1,0:T(4,128)S(1)}, f32[14,4,256]{2,1,0:T(4,128)S(1)}, u32[]{:S(2)}, u32[]{:S(2)}) collective-permute-start(f32[14,4,256]{2,1,0:T(4,128)S(1)} %get-tuple-element.14), channel_id=1, source_target_pairs={{0,3},{1,0},{2,1},{3,2},{4,7},{5,4},{6,5},{7,6},{8,11},{9,8},{10,9... | collective-permute-start | bytes 172040 | tf_op jit(solution)/shard_map/ppermute | solution.py:13
  31.4 5.1 %collective-permute-start.4 = (f32[14,4,256]{2,1,0:T(4,128)S(1)}, f32[14,4,256]{2,1,0:T(4,128)S(1)}, u32[]{:S(2)}, u32[]{:S(2)}) collective-permute-start(f32[14,4,256]{2,1,0:T(4,128)S(1)} %get-tuple-element.15), channel_id=1, source_target_pairs={{0,2},{1,3},{2,0},{3,1},{4,6},{5,7},{6,4},{7,5},{8,10},{9,11},{10,... | collective-permute-start | bytes 172040 | tf_op jit(solution)/shard_map/ppermute | solution.py:13
  31.4 6.0 %collective-permute-start.3 = (f32[14,4,256]{2,1,0:T(4,128)S(1)}, f32[14,4,256]{2,1,0:T(4,128)S(1)}, u32[]{:S(2)}, u32[]{:S(2)}) collective-permute-start(f32[14,4,256]{2,1,0:T(4,128)S(1)} %get-tuple-element.13), channel_id=1, source_target_pairs={{0,1},{1,2},{2,3},{3,0},{4,5},{5,6},{6,7},{7,4},{8,9},{9,10},{10,1... | collective-permute-start | bytes 172040 | tf_op jit(solution)/shard_map/ppermute | solution.py:13

commit v2 on v1

v2 whole, which is shorter than its diff:
```python
import functools

import jax
import jax.numpy as jnp
from jax import lax
from jax.experimental import pallas as pl
from jax.experimental.pallas import tpu as pltpu
from jax.sharding import PartitionSpec as P

ROWS = 4
PRECISION = lax.Precision.HIGHEST


def shifted(value, axis, steps):
    count = lax.axis_size(axis)
    pairs = [(source, (source + steps) % count) for source in range(count)]
    return lax.ppermute(value, axis, pairs)


def sector_steps(sectors):
    return (0, 1, sectors // 2, sectors - 1)


def transform_kernel(here_ref, dims_ref, shift_ref, env_ref, mps_ref, coef_ref,
                     blocks_ref, chosen_ref, masked_sc, left_sc, half_sc):
    sectors = dims_ref.shape[0]
    states = mps_ref.shape[1]
    channels = env_ref.shape[1]
    width = mps_ref.shape[-1]
    here = here_ref[0]
    dims_in = dims_ref[here]
    rows = lax.broadcasted_iota(jnp.int32, (width, width), 0)
    cols = lax.broadcasted_iota(jnp.int32, (width, width), 1)
    for k, step in enumerate(sector_steps(sectors)):
        pick = 0
        for s in range(states):
            pick = pick + jnp.where(lax.rem(shift_ref[s], sectors) == step, s, 0)
        dims_out = dims_ref[lax.rem(here + step, sectors)]
        live = (rows < dims_in) & (cols < dims_out)
        masked = jnp.where(live, mps_ref[0, pick], 0.0)
        masked_sc[k] = masked
        left_sc[k * ROWS:(k + 1) * ROWS, :] = jnp.transpose(masked[:, :128])[:ROWS]
        chosen_ref[k] = coef_ref[pick]
    left = left_sc[...]
    for j in range(channels):
        half = jnp.dot(left, env_ref[0, j], precision=PRECISION,
                       preferred_element_type=jnp.float32)
        for k in range(states):
            half_sc[k, j * ROWS:(j + 1) * ROWS, :] = half[k * ROWS:(k + 1) * ROWS]
    for k in range(states):
        full = jnp.dot(half_sc[k], masked_sc[k], precision=PRECISION,
                       preferred_element_type=jnp.float32)
        for j in range(channels):
            blocks_ref[k, j] = full[j * ROWS:(j + 1) * ROWS]


def transform(here, sector_dims, state_shift, environment, mps, coef_t):
    channels, width = environment.shape[1], environment.shape[-1]
    states = mps.shape[1]
    smem = pl.BlockSpec(memory_space=pltpu.SMEM)
    vmem = pl.BlockSpec(memory_space=pltpu.VMEM)
    flops = 2 * states * ROWS * width * width * channels * 2
    return pl.pallas_call(
        transform_kernel,
        out_shape=(
            jax.ShapeDtypeStruct((states, channels, ROWS, width), jnp.float32),
            jax.ShapeDtypeStruct(coef_t.shape, jnp.float32),
        ),
        in_specs=[smem, smem, smem, vmem, vmem, vmem],
        out_specs=(vmem, vmem),
        scratch_shapes=[
            pltpu.VMEM((states, width, width), jnp.float32),
            pltpu.VMEM((states * ROWS, width), jnp.float32),
            pltpu.VMEM((states, channels * ROWS, width), jnp.float32),
        ],
        compiler_params=pltpu.CompilerParams(vmem_limit_bytes=48 * 1024 * 1024),
        cost_estimate=pl.CostEstimate(
            flops=6 * flops, transcendentals=0,
            bytes_accessed=4 * (environment.size + mps.size + 2 * states * channels * ROWS * width)),
    )(here, sector_dims, state_shift, environment, mps, coef_t)


def local(environment, mps, mpo, mpo_pattern, state_shift, sector_dims):
    highest = lax.Precision.HIGHEST
    sectors = lax.axis_size("sec")
    parts = lax.axis_size("op")
    me = lax.axis_index("op")
    here = lax.axis_index("sec").astype(jnp.int32).reshape(1)
    coef_t = jnp.transpose(mpo * mpo_pattern[:, :, None].astype(jnp.float32), (1, 0, 2))
    blocks, chosen = transform(here, sector_dims, state_shift, environment, mps, coef_t)
    routed = [blocks[0]]
    for k, step in enumerate(sector_steps(sectors)):
        if k:
            routed.append(shifted(blocks[k], "sec", step))
    partial = jnp.einsum("kwrc,kwv->vrc", jnp.stack(routed), chosen, precision=highest)
    chunk = partial.shape[0] // parts
    pieces = partial.reshape((parts, chunk) + partial.shape[1:])
    total = lax.dynamic_index_in_dim(pieces, me, 0, keepdims=False)
    for step in range(1, parts):
        send = lax.dynamic_index_in_dim(pieces, (me + step) % parts, 0, keepdims=False)
        total = total + shifted(send, "op", step)
    return total[None]


def solution(mesh):
    in_specs = (
        P("sec", "op", None, None),
        P("sec", None, None, None),
        P("op", None, None),
        P("op", None),
        P(),
        P(),
    )
    out_specs = P("sec", "op", None, None)
    return jax.shard_map(local, mesh=mesh, in_specs=in_specs, out_specs=out_specs, check_vma=False)
```

time: 38.3 us -> 28.7 us (0.75)
  between operations: 7.71 us -> 0.06 us
  matrix products: 5.42 us -> 0.39 us
  Pallas kernels: 0 us -> 3.05 us
  other arithmetic: 5.19 us -> 2.21 us
  local copies, waits for them, and re-layouts: 1.85 us -> 4.71 us
    dot_general x2 -> x0, matrix products: 5.02 us -> none  [the longest x1 3.91 us: local(): half = jnp.einsum('sar,wab->swrb', left, environment[0], precision=highest)]
    pallas_call x0 -> x1, Pallas kernels: none -> 3.05 us  [transform(): pl.pallas_call(transform_kernel, out_shape=(jax.ShapeDtypeStruct((states,...]
    unnamed x5 -> x8, local copies, waits for them, and re-layouts: 1.57 us -> 4.57 us
    reduce_sum x3 -> x0, other arithmetic: 2.87 us -> none  [the longest x1 1.29 us: local(): dims_in = jnp.sum(jnp.where(labels == here, sector_dims, 0))]
    transpose x0 -> x1, other arithmetic: none -> 0.82 us  [local(): jnp.transpose(mpo * mpo_pattern[:, :, None].astype(jnp.float32), (1, 0, 2))]
    select_n x1 -> x0, other arithmetic: 0.66 us -> none  [local(): state_shift % sectors == step]
  transfers between devices with their start and end apart: 6 -> 6, of which waited for: 6 -> 6; matrix products, arithmetic and copies ran while one was open for 1% -> 0% of each run, Pallas kernels for 0% -> 0%
where the time goes in v2:
time: 28.7 us; the launch traced here: 28.4 us
  waiting for transfers between devices  9.46 us (33%)
  starting transfers between devices  8.57 us (30%)
  local copies, waits for them, and re-layouts  4.71 us (16%)
  Pallas kernels  3.05 us (11%)
  other arithmetic  2.21 us (8%)
  matrix products  0.39 us (1%)
    ppermute x6, waiting for transfers between devices, shifted(): return lax.ppermute(value, axis, pairs)  9.46 us
    ppermute x6, starting transfers between devices, shifted(): return lax.ppermute(value, axis, pairs)  8.57 us
    unnamed x8, local copies, waits for them, and re-layouts  4.57 us
    pallas_call x1, Pallas kernels, transform(): pl.pallas_call(transform_kernel, out_shape=(jax.ShapeDtypeStruct((states,...  3.05 us
    transpose x1, other arithmetic, local(): jnp.transpose(mpo * mpo_pattern[:, :, None].astype(jnp.float32), (1, 0, 2))  0.82 us
    convert_element_type x1, other arithmetic, local(): mpo_pattern[:, :, None].astype(jnp.float32)  0.68 us
    broadcast_in_dim x1, other arithmetic, local(): return total[None]  0.66 us
  transfers between devices with their start and end apart: 6, of which 6 were waited for; matrix products, arithmetic and copies ran while one was open for 0% of the time, Pallas kernels for 0%

profile of v2, /device:TPU:0, one launch (start us, length us, event | category | flops | bytes accessed | tf_op | source)
XLA Modules:
  0.0 28.4 jit_solution(15098339875190318076)
XLA Ops:
  0.0 0.7 %convert_element_type.4 = f32[14,4]{0,1:T(4,128)S(1)} convert(s32[14,4]{0,1:T(4,128)} %param.9) | non-fusion elementwise | flops 56 | bytes 448 | tf_op jit(solution)/shard_map/convert_element_type | solution.py:89
  0.7 0.8 %fusion.5.coef_ref = f32[4,14,56]{2,1,0:T(8,128)S(1)} fusion(f32[14,4,56]{2,1,0:T(4,128)} %param.8, f32[14,4]{0,1:T(4,128)S(1)} %convert_element_type.4), kind=kLoop, calls=%fused_computation.15 | loop fusion | flops 3136 | bytes 25312 | tf_op jit(solution)/shard_map/transpose | solution.py:89
  1.5 0.0 copy-start
  1.5 2.0 %copy-done = f32[1,14,256,256]{3,2,1,0:T(8,128)S(1)} copy-done((f32[1,14,256,256]{3,2,1,0:T(8,128)S(1)}, f32[1,14,256,256]{3,2,1,0:T(8,128)}, u32[]{:S(2)}) %copy-start) | copy-done | bytes 3670040
  3.5 0.0 copy-start.1
  3.5 1.2 %copy-done.1 = f32[1,4,256,256]{3,2,1,0:T(8,128)S(1)} copy-done((f32[1,4,256,256]{3,2,1,0:T(8,128)S(1)}, f32[1,4,256,256]{3,2,1,0:T(8,128)}, u32[]{:S(2)}) %copy-start.1) | copy-done | bytes 1048600
  4.8 0.0 copy-start.2
  4.8 0.7 %copy-done.2 = s32[8]{0:T(128)S(1)} copy-done((s32[8]{0:T(128)S(1)}, s32[8]{0:T(128)}, u32[]{:S(2)}) %copy-start.2) | copy-done | bytes 56
  5.4 0.0 copy-start.3
  5.4 0.7 %copy-done.3 = s32[4]{0:T(128)S(1)} copy-done((s32[4]{0:T(128)S(1)}, s32[4]{0:T(128)}, u32[]{:S(2)}) %copy-start.3) | copy-done | bytes 40
  6.1 3.0 %shard_map.64 = (f32[4,14,4,256]{3,2,1,0:T(4,128)S(1)}, f32[4,14,56]{2,1,0:T(8,128)S(1)}) custom-call(s32[1]{0:T(128)} %bitcast.here_ref, s32[8]{0:T(128)S(1)} %copy-done.2, s32[4]{0:T(128)S(1)} %copy-done.3, f32[1,14,256,256]{3,2,1,0:T(8,128)S(1)} %copy-done, f32[1,4,256,256]{3,2,1,0:T(8,128)S(1)} %copy-done.1, f32[4,14,56]{2,1,0:T(8,128)S(1)} %fusion.5.coef_ref), custom_call_target="tpu_custom_call" | custom-call | flops 352321536 | bytes 5177344 | tf_op jit(solution)/shard_map/pallas_call | solution.py:63
  9.2 3.4 %collective-permute-start.2 = (f32[14,4,256]{2,1,0:T(4,128)S(1)}, f32[14,4,256]{2,1,0:T(4,128)S(1)}, u32[]{:S(2)}, u32[]{:S(2)}) collective-permute-start(f32[14,4,256]{2,1,0:T(4,128)S(1)} %get-tuple-element.13), channel_id=1, source_target_pairs={{0,28},{4,0},{8,4},{12,8},{16,12},{20,16},{24,20},{28,24},{1,29},{... | collective-permute-start | bytes 172040 | tf_op jit(solution)/shard_map/ppermute | solution.py:17
  12.6 0.5 %collective-permute-start.1 = (f32[14,4,256]{2,1,0:T(4,128)S(1)}, f32[14,4,256]{2,1,0:T(4,128)S(1)}, u32[]{:S(2)}, u32[]{:S(2)}) collective-permute-start(f32[14,4,256]{2,1,0:T(4,128)S(1)} %get-tuple-element.14), channel_id=1, source_target_pairs={{0,16},{4,20},{8,24},{12,28},{16,0},{20,4},{24,8},{28,12},{1,17},{... | collective-permute-start | bytes 172040 | tf_op jit(solution)/shard_map/ppermute | solution.py:17
  13.1 0.0 collective-permute-start
  13.1 1.3 %collective-permute-done.2 = f32[14,4,256]{2,1,0:T(4,128)S(1)} collective-permute-done((f32[14,4,256]{2,1,0:T(4,128)S(1)}, f32[14,4,256]{2,1,0:T(4,128)S(1)}, u32[]{:S(2)}, u32[]{:S(2)}) %collective-permute-start.2) | collective-permute-done | bytes 57376 | tf_op jit(solution)/shard_map/ppermute | solution.py:17
  14.4 2.3 %collective-permute-done.1 = f32[14,4,256]{2,1,0:T(4,128)S(1)} collective-permute-done((f32[14,4,256]{2,1,0:T(4,128)S(1)}, f32[14,4,256]{2,1,0:T(4,128)S(1)}, u32[]{:S(2)}, u32[]{:S(2)}) %collective-permute-start.1) | collective-permute-done | bytes 57376 | tf_op jit(solution)/shard_map/ppermute | solution.py:17
  16.7 0.8 %collective-permute-done = f32[14,4,256]{2,1,0:T(4,128)S(1)} collective-permute-done((f32[14,4,256]{2,1,0:T(4,128)S(1)}, f32[14,4,256]{2,1,0:T(4,128)S(1)}, u32[]{:S(2)}, u32[]{:S(2)}) %collective-permute-start) | collective-permute-done | bytes 57376 | tf_op jit(solution)/shard_map/ppermute | solution.py:17
  17.6 0.1 pad_maximum_fusion
  17.6 0.4 %convolution_bitcast_fusion = f32[56,4,256]{2,0,1:T(8,128)S(1)} fusion(f32[4,14,4,256]{3,2,1,0:T(4,128)S(1)} %pad_maximum_fusion, f32[4,14,56]{2,1,0:T(8,128)S(1)} %get-tuple-element.7), kind=kOutput, calls=%fused_computation | convolution fusion | flops 38535168 | bytes 471296 | tf_op jit(solution)/shard_map/kwrc,kwv->vrc/dot_general | solution.py:95
  18.0 0.1 copy.15
  18.2 3.7 %collective-permute-start.5 = (f32[14,4,256]{2,1,0:T(4,128)S(1)}, f32[14,4,256]{2,1,0:T(4,128)S(1)}, u32[]{:S(2)}, u32[]{:S(2)}) collective-permute-start(f32[14,4,256]{2,1,0:T(4,128)S(1)} %get-tuple-element.10), channel_id=1, source_target_pairs={{0,3},{1,0},{2,1},{3,2},{4,7},{5,4},{6,5},{7,6},{8,11},{9,8},{10,9... | collective-permute-start | bytes 172040 | tf_op jit(solution)/shard_map/ppermute | solution.py:17
  21.8 0.0 collective-permute-start.4
  21.8 1.0 %collective-permute-start.3 = (f32[14,4,256]{2,1,0:T(4,128)S(1)}, f32[14,4,256]{2,1,0:T(4,128)S(1)}, u32[]{:S(2)}, u32[]{:S(2)}) collective-permute-start(f32[14,4,256]{2,1,0:T(4,128)S(1)} %get-tuple-element.9), channel_id=1, source_target_pairs={{0,1},{1,2},{2,3},{3,0},{4,5},{5,6},{6,7},{7,4},{8,9},{9,10},{10,1... | collective-permute-start | bytes 172040 | tf_op jit(solution)/shard_map/ppermute | solution.py:17
  22.8 0.8 %collective-permute-done.5 = f32[14,4,256]{2,1,0:T(4,128)S(1)} collective-permute-done((f32[14,4,256]{2,1,0:T(4,128)S(1)}, f32[14,4,256]{2,1,0:T(4,128)S(1)}, u32[]{:S(2)}, u32[]{:S(2)}) %collective-permute-start.5) | collective-permute-done | bytes 57376 | tf_op jit(solution)/shard_map/ppermute | solution.py:17
  23.6 3.2 %collective-permute-done.4 = f32[14,4,256]{2,1,0:T(4,128)S(1)} collective-permute-done((f32[14,4,256]{2,1,0:T(4,128)S(1)}, f32[14,4,256]{2,1,0:T(4,128)S(1)}, u32[]{:S(2)}, u32[]{:S(2)}) %collective-permute-start.4) | collective-permute-done | bytes 57376 | tf_op jit(solution)/shard_map/ppermute | solution.py:17
  26.9 0.9 %collective-permute-done.3 = f32[14,4,256]{2,1,0:T(4,128)S(1)} collective-permute-done((f32[14,4,256]{2,1,0:T(4,128)S(1)}, f32[14,4,256]{2,1,0:T(4,128)S(1)}, u32[]{:S(2)}, u32[]{:S(2)}) %collective-permute-start.3) | collective-permute-done | bytes 57376 | tf_op jit(solution)/shard_map/ppermute | solution.py:17
  27.8 0.7 %fusion.3 = f32[1,14,4,256]{3,2,1,0:T(4,128)} fusion(f32[14,4,256]{2,1,0:T(4,128)S(1)} %collective-permute-done.5, f32[14,4,256]{2,1,0:T(4,128)S(1)} %collective-permute-done.4, f32[14,4,256]{2,1,0:T(4,128)S(1)} %collective-permute-done.3, f32[4,14,4,256]{3,2,1,0:T(4,128)S(1)} %bitcast.36, s32[]{:T(128)S(6)} %select_n.28), kind=kLoop, calls=%fused_computation.6 | loop fusion | flops 43008 | bytes 286724 | tf_op jit(solution)/shard_map/broadcast_in_dim | solution.py:102
  (2 shorter events, 0.0 us)
Async XLA Ops:
  1.5 2.0 %copy-start = (f32[1,14,256,256]{3,2,1,0:T(8,128)S(1)}, f32[1,14,256,256]{3,2,1,0:T(8,128)}, u32[]{:S(2)}) copy-start(f32[1,14,256,256]{3,2,1,0:T(8,128)} %env_ref.1) | copy-start | bytes 11010052
  3.5 1.2 %copy-start.1 = (f32[1,4,256,256]{3,2,1,0:T(8,128)S(1)}, f32[1,4,256,256]{3,2,1,0:T(8,128)}, u32[]{:S(2)}) copy-start(f32[1,4,256,256]{3,2,1,0:T(8,128)} %mps_ref.1) | copy-start | bytes 3145732
  4.8 0.7 %copy-start.2 = (s32[8]{0:T(128)S(1)}, s32[8]{0:T(128)}, u32[]{:S(2)}) copy-start(s32[8]{0:T(128)} %dims_ref.1) | copy-start | bytes 100
  5.4 0.7 %copy-start.3 = (s32[4]{0:T(128)S(1)}, s32[4]{0:T(128)}, u32[]{:S(2)}) copy-start(s32[4]{0:T(128)} %shift_ref.1) | copy-start | bytes 52
  9.2 5.2 %collective-permute-start.2 = (f32[14,4,256]{2,1,0:T(4,128)S(1)}, f32[14,4,256]{2,1,0:T(4,128)S(1)}, u32[]{:S(2)}, u32[]{:S(2)}) collective-permute-start(f32[14,4,256]{2,1,0:T(4,128)S(1)} %get-tuple-element.13), channel_id=1, source_target_pairs={{0,28},{4,0},{8,4},{12,8},{16,12},{20,16},{24,20},{28,24},{1,29},{... | collective-permute-start | bytes 172040 | tf_op jit(solution)/shard_map/ppermute | solution.py:17
  12.6 4.2 %collective-permute-start.1 = (f32[14,4,256]{2,1,0:T(4,128)S(1)}, f32[14,4,256]{2,1,0:T(4,128)S(1)}, u32[]{:S(2)}, u32[]{:S(2)}) collective-permute-start(f32[14,4,256]{2,1,0:T(4,128)S(1)} %get-tuple-element.14), channel_id=1, source_target_pairs={{0,16},{4,20},{8,24},{12,28},{16,0},{20,4},{24,8},{28,12},{1,17},{... | collective-permute-start | bytes 172040 | tf_op jit(solution)/shard_map/ppermute | solution.py:17
  13.1 4.5 %collective-permute-start = (f32[14,4,256]{2,1,0:T(4,128)S(1)}, f32[14,4,256]{2,1,0:T(4,128)S(1)}, u32[]{:S(2)}, u32[]{:S(2)}) collective-permute-start(f32[14,4,256]{2,1,0:T(4,128)S(1)} %get-tuple-element.15), channel_id=1, source_target_pairs={{0,4},{4,8},{8,12},{12,16},{16,20},{20,24},{24,28},{28,0},{1,5},{5... | collective-permute-start | bytes 172040 | tf_op jit(solution)/shard_map/ppermute | solution.py:17
  18.2 5.5 %collective-permute-start.5 = (f32[14,4,256]{2,1,0:T(4,128)S(1)}, f32[14,4,256]{2,1,0:T(4,128)S(1)}, u32[]{:S(2)}, u32[]{:S(2)}) collective-permute-start(f32[14,4,256]{2,1,0:T(4,128)S(1)} %get-tuple-element.10), channel_id=1, source_target_pairs={{0,3},{1,0},{2,1},{3,2},{4,7},{5,4},{6,5},{7,6},{8,11},{9,8},{10,9... | collective-permute-start | bytes 172040 | tf_op jit(solution)/shard_map/ppermute | solution.py:17
  21.8 5.1 %collective-permute-start.4 = (f32[14,4,256]{2,1,0:T(4,128)S(1)}, f32[14,4,256]{2,1,0:T(4,128)S(1)}, u32[]{:S(2)}, u32[]{:S(2)}) collective-permute-start(f32[14,4,256]{2,1,0:T(4,128)S(1)} %get-tuple-element.11), channel_id=1, source_target_pairs={{0,2},{1,3},{2,0},{3,1},{4,6},{5,7},{6,4},{7,5},{8,10},{9,11},{10,... | collective-permute-start | bytes 172040 | tf_op jit(solution)/shard_map/ppermute | solution.py:17
  21.8 6.0 %collective-permute-start.3 = (f32[14,4,256]{2,1,0:T(4,128)S(1)}, f32[14,4,256]{2,1,0:T(4,128)S(1)}, u32[]{:S(2)}, u32[]{:S(2)}) collective-permute-start(f32[14,4,256]{2,1,0:T(4,128)S(1)} %get-tuple-element.9), channel_id=1, source_target_pairs={{0,1},{1,2},{2,3},{3,0},{4,5},{5,6},{6,7},{7,4},{8,9},{9,10},{10,1... | collective-permute-start | bytes 172040 | tf_op jit(solution)/shard_map/ppermute | solution.py:17

commit v3 on v2

v3 whole, which is shorter than its diff:
```python
import jax
import jax.numpy as jnp
from jax import lax
from jax.experimental import pallas as pl
from jax.experimental.pallas import tpu as pltpu
from jax.sharding import PartitionSpec as P

ROWS = 4
PRECISION = lax.Precision.HIGHEST


def shifted(value, axis, steps):
    count = lax.axis_size(axis)
    pairs = [(source, (source + steps) % count) for source in range(count)]
    return lax.ppermute(value, axis, pairs)


def sector_steps(sectors):
    return (0, 1, sectors // 2, sectors - 1)


def transform_kernel(dims_hbm, shift_hbm, env_hbm, mps_hbm, *refs):
    count = len(refs) - 8
    onehot_ref, dims_sc, shift_sc, mps_sc, env_sc, masked_sc, left_sc, half_sc, sems = refs[count - 1:]
    blocks_refs = refs[:count - 1]
    sectors = dims_sc.shape[0]
    states = mps_sc.shape[0]
    channels = env_sc.shape[0]
    width = mps_sc.shape[-1]
    small = [
        pltpu.make_async_copy(dims_hbm, dims_sc, sems.at[0]),
        pltpu.make_async_copy(shift_hbm, shift_sc, sems.at[1]),
        pltpu.make_async_copy(mps_hbm.at[0], mps_sc, sems.at[2]),
    ]
    for copy in small:
        copy.start()
    loads = []
    for j in range(channels):
        copy = pltpu.make_async_copy(env_hbm.at[0, j], env_sc.at[j], sems.at[3 + j])
        copy.start()
        loads.append(copy)
    for copy in small:
        copy.wait()
    here = lax.axis_index("sec")
    dims_in = dims_sc[here]
    rows = lax.broadcasted_iota(jnp.int32, (width, width), 0)
    cols = lax.broadcasted_iota(jnp.int32, (width, width), 1)
    lanes = lax.broadcasted_iota(jnp.int32, (1, states), 1)
    for k, step in enumerate(sector_steps(sectors)):
        pick = 0
        for s in range(states):
            pick = pick + jnp.where(lax.rem(shift_sc[s], sectors) == step, s, 0)
        dims_out = dims_sc[lax.rem(here + step, sectors)]
        live = (rows < dims_in) & (cols < dims_out)
        masked = jnp.where(live, mps_sc[pick], 0.0)
        masked_sc[k] = masked
        left_sc[k * ROWS:(k + 1) * ROWS, :] = jnp.transpose(masked[:, :128])[:ROWS]
        onehot_ref[k:k + 1, :] = (lanes == pick).astype(jnp.float32)
    left = left_sc[...]
    for j in range(channels):
        loads[j].wait()
        half = jnp.dot(left, env_sc[j], precision=PRECISION,
                       preferred_element_type=jnp.float32)
        for k in range(states):
            half_sc[k, j * ROWS:(j + 1) * ROWS, :] = half[k * ROWS:(k + 1) * ROWS]
    for k in range(states):
        full = jnp.dot(half_sc[k], masked_sc[k], precision=PRECISION,
                       preferred_element_type=jnp.float32)
        for j in range(channels):
            blocks_refs[k][j] = full[j * ROWS:(j + 1) * ROWS]


def transform(sector_dims, state_shift, environment, mps):
    channels, width = environment.shape[1], environment.shape[-1]
    states = mps.shape[1]
    anywhere = pl.BlockSpec(memory_space=pl.ANY)
    vmem = pl.BlockSpec(memory_space=pltpu.VMEM)
    flops = 2 * states * ROWS * width * width * channels * 2
    return pl.pallas_call(
        transform_kernel,
        out_shape=tuple(
            jax.ShapeDtypeStruct((channels, ROWS, width), jnp.float32) for _ in range(states)
        ) + (jax.ShapeDtypeStruct((states, states), jnp.float32),),
        in_specs=[anywhere] * 4,
        out_specs=(vmem,) * (states + 1),
        scratch_shapes=[
            pltpu.SMEM(sector_dims.shape, jnp.int32),
            pltpu.SMEM(state_shift.shape, jnp.int32),
            pltpu.VMEM((states, width, width), jnp.float32),
            pltpu.VMEM((channels, width, width), jnp.float32),
            pltpu.VMEM((states, width, width), jnp.float32),
            pltpu.VMEM((states * ROWS, width), jnp.float32),
            pltpu.VMEM((states, channels * ROWS, width), jnp.float32),
            pltpu.SemaphoreType.DMA((3 + channels,)),
        ],
        cost_estimate=pl.CostEstimate(
            flops=6 * flops, transcendentals=0,
            bytes_accessed=4 * (environment.size + mps.size + states * channels * ROWS * width)),
    )(sector_dims, state_shift, environment, mps)


def local(environment, mps, mpo, mpo_pattern, state_shift, sector_dims):
    highest = lax.Precision.HIGHEST
    sectors = lax.axis_size("sec")
    parts = lax.axis_size("op")
    me = lax.axis_index("op")
    *blocks, onehot = transform(sector_dims, state_shift, environment, mps)
    routed = [blocks[0]]
    for k, step in enumerate(sector_steps(sectors)):
        if k:
            routed.append(shifted(blocks[k], "sec", step))
    coef = mpo * mpo_pattern[:, :, None].astype(jnp.float32)
    chosen = jnp.sum(onehot[:, None, :, None] * coef[None], axis=2)
    partial = jnp.einsum("kwrc,kwv->vrc", jnp.stack(routed), chosen, precision=highest)
    chunk = partial.shape[0] // parts
    pieces = partial.reshape((parts, chunk) + partial.shape[1:])
    total = lax.dynamic_index_in_dim(pieces, me, 0, keepdims=False)
    for step in range(1, parts):
        send = lax.dynamic_index_in_dim(pieces, (me + step) % parts, 0, keepdims=False)
        total = total + shifted(send, "op", step)
    return total[None]


def solution(mesh):
    in_specs = (
        P("sec", "op", None, None),
        P("sec", None, None, None),
        P("op", None, None),
        P("op", None),
        P(),
        P(),
    )
    out_specs = P("sec", "op", None, None)
    return jax.shard_map(local, mesh=mesh, in_specs=in_specs, out_specs=out_specs, check_vma=False)
```

time: 28.7 us -> 28.1 us (0.979)
  local copies, waits for them, and re-layouts: 4.71 us -> 0.36 us
  Pallas kernels: 3.05 us -> 7.39 us
  waiting for transfers between devices: 9.46 us -> 8.49 us
    unnamed x8 -> x4, local copies, waits for them, and re-layouts: 4.57 us -> 0.01 us
    pallas_call x1, Pallas kernels: 3.05 us -> 7.39 us  [transform(): pl.pallas_call(transform_kernel, out_shape=tuple((jax.ShapeDtypeStruct((c...]
    ppermute x6, waiting for transfers between devices: 9.46 us -> 8.49 us  [shifted(): return lax.ppermute(value, axis, pairs)]
    reduce_sum x0 -> x1, other arithmetic: none -> 0.82 us  [local(): chosen = jnp.sum(onehot[:, None, :, None] * coef[None], axis=2)]
    transpose x1 -> x0, other arithmetic: 0.82 us -> none  [local(): jnp.transpose(mpo * mpo_pattern[:, :, None].astype(jnp.float32), (1, 0, 2))]
    another operation x1, other arithmetic: 0.05 us -> 0.87 us  [local(): jnp.stack(routed)]
    convert_element_type x1, other arithmetic: 0.68 us -> 0.01 us  [local(): coef = mpo * mpo_pattern[:, :, None].astype(jnp.float32)]
  transfers between devices with their start and end apart: 6 -> 6, of which waited for: 6 -> 6; matrix products, arithmetic and copies ran while one was open for 0% -> 4% of each run, Pallas kernels for 0% -> 0%
where the time goes in v3:
time: 28.1 us; the launch traced here: 28 us
  starting transfers between devices  8.67 us (31%)
  waiting for transfers between devices  8.49 us (30%)
  Pallas kernels  7.39 us (26%)
  other arithmetic  2.46 us (9%)
  matrix products  0.44 us (2%)
  local copies, waits for them, and re-layouts  0.36 us (1%)
    ppermute x6, starting transfers between devices, shifted(): return lax.ppermute(value, axis, pairs)  8.67 us
    ppermute x6, waiting for transfers between devices, shifted(): return lax.ppermute(value, axis, pairs)  8.49 us
    pallas_call x1, Pallas kernels, transform(): pl.pallas_call(transform_kernel, out_shape=tuple((jax.ShapeDtypeStruct((c...  7.39 us
    another operation x1, other arithmetic, local(): jnp.stack(routed)  0.87 us
    reduce_sum x1, other arithmetic, local(): chosen = jnp.sum(onehot[:, None, :, None] * coef[None], axis=2)  0.82 us
    broadcast_in_dim x1, other arithmetic, local(): return total[None]  0.68 us
  transfers between devices with their start and end apart: 6, of which 6 were waited for; matrix products, arithmetic and copies ran while one was open for 4% of the time, Pallas kernels for 0%

profile of v3, /device:TPU:0, one launch (start us, length us, event | category | flops | bytes accessed | tf_op | source)
XLA Modules:
  0.0 28.0 jit_solution(3399191220192843752)
XLA Ops:
  0.0 0.0 copy-start.1
  0.0 0.0 copy-start
  0.0 7.4 %shard_map.64 = (f32[14,4,256]{2,1,0:T(4,128)}, f32[14,4,256]{2,1,0:T(4,128)}, f32[14,4,256]{2,1,0:T(4,128)}, f32[14,4,256]{2,1,0:T(4,128)}, f32[4,4]{1,0:T(4,128)}) custom-call(s32[8]{0:T(128)} %dims_hbm.1, s32[4]{0:T(128)} %shift_hbm.1, f32[1,14,256,256]{3,2,1,0:T(8,128)} %env_hbm.1, f32[1,4,256,256]{3,2,1,0:T(8,128)} %mps_hbm.1), custom_call_target="tpu_custom_call" | custom-call | flops 352321536 | bytes 4947968 | tf_op jit(solution)/shard_map/pallas_call | solution.py:79
  7.4 3.4 %collective-permute-start.2 = (f32[14,4,256]{2,1,0:T(4,128)}, f32[14,4,256]{2,1,0:T(4,128)S(1)}, u32[]{:S(2)}, u32[]{:S(2)}) collective-permute-start(f32[14,4,256]{2,1,0:T(4,128)} %get-tuple-element.14), channel_id=1, source_target_pairs={{0,28},{4,0},{8,4},{12,8},{16,12},{20,16},{24,20},{28,24},{1,29},{... | collective-permute-start | bytes 172040 | tf_op jit(solution)/shard_map/ppermute | solution.py:15
  10.8 0.5 %collective-permute-start.1 = (f32[14,4,256]{2,1,0:T(4,128)}, f32[14,4,256]{2,1,0:T(4,128)S(1)}, u32[]{:S(2)}, u32[]{:S(2)}) collective-permute-start(f32[14,4,256]{2,1,0:T(4,128)} %get-tuple-element.13), channel_id=1, source_target_pairs={{0,16},{4,20},{8,24},{12,28},{16,0},{20,4},{24,8},{28,12},{1,17},{... | collective-permute-start | bytes 172040 | tf_op jit(solution)/shard_map/ppermute | solution.py:15
  11.3 0.0 collective-permute-start
  11.3 0.0 copy-done.1
  11.3 0.1 copy.16
  11.4 0.0 copy-done
  11.4 0.1 broadcast_multiply_fusion
  11.5 0.8 %multiply_reduce_fusion = f32[4,14,56]{2,1,0:T(8,128)S(1)} fusion(f32[14,4,56]{2,1,0:T(4,128)S(1)} %broadcast_multiply_fusion, f32[4,4]{1,0:T(4,128)} %get-tuple-element.10), kind=kLoop, calls=%fused_computation.5 | loop fusion | flops 21952 | bytes 25152 | tf_op jit(solution)/shard_map/reduce_sum | solution.py:113
  12.4 0.1 reshape.9
  12.5 0.4 %collective-permute-done.2 = f32[14,4,256]{2,1,0:T(4,128)S(1)} collective-permute-done((f32[14,4,256]{2,1,0:T(4,128)}, f32[14,4,256]{2,1,0:T(4,128)S(1)}, u32[]{:S(2)}, u32[]{:S(2)}) %collective-permute-start.2) | collective-permute-done | bytes 57376 | tf_op jit(solution)/shard_map/ppermute | solution.py:15
  12.9 2.2 %collective-permute-done.1 = f32[14,4,256]{2,1,0:T(4,128)S(1)} collective-permute-done((f32[14,4,256]{2,1,0:T(4,128)}, f32[14,4,256]{2,1,0:T(4,128)S(1)}, u32[]{:S(2)}, u32[]{:S(2)}) %collective-permute-start.1) | collective-permute-done | bytes 57376 | tf_op jit(solution)/shard_map/ppermute | solution.py:15
  15.2 0.8 %collective-permute-done = f32[14,4,256]{2,1,0:T(4,128)S(1)} collective-permute-done((f32[14,4,256]{2,1,0:T(4,128)}, f32[14,4,256]{2,1,0:T(4,128)S(1)}, u32[]{:S(2)}, u32[]{:S(2)}) %collective-permute-start) | collective-permute-done | bytes 57376 | tf_op jit(solution)/shard_map/ppermute | solution.py:15
  16.0 0.9 %pad_maximum_fusion = f32[4,14,4,256]{3,2,1,0:T(4,128)S(1)} fusion(f32[1,14,4,256]{3,2,1,0:T(4,128)S(1)} %bitcast.36, f32[1,14,4,256]{3,2,1,0:T(4,128)S(1)} %bitcast.37, f32[1,14,4,256]{3,2,1,0:T(4,128)S(1)} %bitcast.38, f32[1,14,4,256]{3,2,1,0:T(4,128)} %bitcast.35), kind=kLoop, calls=%fused_computation.3 | loop fusion | flops 172032 | bytes 458752 | tf_op jit(solution)/shard_map/stack | solution.py:114
  16.9 0.4 %convolution_bitcast_fusion = f32[4,14,4,256]{3,1,2,0:T(8,128)S(1)} fusion(f32[4,14,4,256]{3,2,1,0:T(4,128)S(1)} %pad_maximum_fusion, f32[4,14,4,14,1]{1,0,3,2,4:T(4,128)S(1)} %bitcast.33), kind=kOutput, calls=%fused_computation | convolution fusion | flops 38535168 | bytes 471296 | tf_op jit(solution)/shard_map/kwrc,kwv->vrc/dot_general | solution.py:114
  17.4 3.7 %collective-permute-start.5 = (f32[14,4,256]{2,1,0:T(4,128)S(1)}, f32[14,4,256]{2,1,0:T(4,128)S(1)}, u32[]{:S(2)}, u32[]{:S(2)}) collective-permute-start(f32[14,4,256]{2,1,0:T(4,128)S(1)} %bitcast.39), channel_id=1, source_target_pairs={{0,3},{1,0},{2,1},{3,2},{4,7},{5,4},{6,5},{7,6},{8,11},{9,8},{10,9... | collective-permute-start | bytes 172040 | tf_op jit(solution)/shard_map/ppermute | solution.py:15
  21.1 0.1 collective-permute-start.4
  21.2 1.0 %collective-permute-start.3 = (f32[14,4,256]{2,1,0:T(4,128)S(1)}, f32[14,4,256]{2,1,0:T(4,128)S(1)}, u32[]{:S(2)}, u32[]{:S(2)}) collective-permute-start(f32[14,4,256]{2,1,0:T(4,128)S(1)} %bitcast.41), channel_id=1, source_target_pairs={{0,1},{1,2},{2,3},{3,0},{4,5},{5,6},{6,7},{7,4},{8,9},{9,10},{10,1... | collective-permute-start | bytes 172040 | tf_op jit(solution)/shard_map/ppermute | solution.py:15
  22.3 0.6 %collective-permute-done.5 = f32[14,4,256]{2,1,0:T(4,128)S(1)} collective-permute-done((f32[14,4,256]{2,1,0:T(4,128)S(1)}, f32[14,4,256]{2,1,0:T(4,128)S(1)}, u32[]{:S(2)}, u32[]{:S(2)}) %collective-permute-start.5) | collective-permute-done | bytes 57376 | tf_op jit(solution)/shard_map/ppermute | solution.py:15
  22.9 3.4 %collective-permute-done.4 = f32[14,4,256]{2,1,0:T(4,128)S(1)} collective-permute-done((f32[14,4,256]{2,1,0:T(4,128)S(1)}, f32[14,4,256]{2,1,0:T(4,128)S(1)}, u32[]{:S(2)}, u32[]{:S(2)}) %collective-permute-start.4) | collective-permute-done | bytes 57376 | tf_op jit(solution)/shard_map/ppermute | solution.py:15
  26.3 1.0 %collective-permute-done.3 = f32[14,4,256]{2,1,0:T(4,128)S(1)} collective-permute-done((f32[14,4,256]{2,1,0:T(4,128)S(1)}, f32[14,4,256]{2,1,0:T(4,128)S(1)}, u32[]{:S(2)}, u32[]{:S(2)}) %collective-permute-start.3) | collective-permute-done | bytes 57376 | tf_op jit(solution)/shard_map/ppermute | solution.py:15
  27.3 0.7 %fusion.5 = f32[1,14,4,256]{3,2,1,0:T(4,128)} fusion(f32[14,4,256]{2,1,0:T(4,128)S(1)} %collective-permute-done.5, f32[14,4,256]{2,1,0:T(4,128)S(1)} %collective-permute-done.4, f32[14,4,256]{2,1,0:T(4,128)S(1)} %collective-permute-done.3, f32[1,14,4,256]{3,1,2,0:T(8,128)S(1)} %get-tuple-element.15), kind=kLoop, calls=%fused_computation.9 | loop fusion | flops 43008 | bytes 286720 | tf_op jit(solution)/shard_map/broadcast_in_dim | solution.py:121
  (5 shorter events, 0.2 us)
Async XLA Ops:
  0.0 11.3 %copy-start.1 = (s32[14,4]{0,1:T(4,128)S(1)}, s32[14,4]{0,1:T(4,128)}, u32[]{:S(2)}) copy-start(s32[14,4]{0,1:T(4,128)} %param.9) | copy-start | bytes 676
  0.0 11.4 %copy-start = (f32[14,4,56]{2,1,0:T(4,128)S(1)}, f32[14,4,56]{2,1,0:T(4,128)}, u32[]{:S(2)}) copy-start(f32[14,4,56]{2,1,0:T(4,128)} %param.8) | copy-start | bytes 37636
  7.4 5.5 %collective-permute-start.2 = (f32[14,4,256]{2,1,0:T(4,128)}, f32[14,4,256]{2,1,0:T(4,128)S(1)}, u32[]{:S(2)}, u32[]{:S(2)}) collective-permute-start(f32[14,4,256]{2,1,0:T(4,128)} %get-tuple-element.14), channel_id=1, source_target_pairs={{0,28},{4,0},{8,4},{12,8},{16,12},{20,16},{24,20},{28,24},{1,29},{... | collective-permute-start | bytes 172040 | tf_op jit(solution)/shard_map/ppermute | solution.py:15
  10.8 4.4 %collective-permute-start.1 = (f32[14,4,256]{2,1,0:T(4,128)}, f32[14,4,256]{2,1,0:T(4,128)S(1)}, u32[]{:S(2)}, u32[]{:S(2)}) collective-permute-start(f32[14,4,256]{2,1,0:T(4,128)} %get-tuple-element.13), channel_id=1, source_target_pairs={{0,16},{4,20},{8,24},{12,28},{16,0},{20,4},{24,8},{28,12},{1,17},{... | collective-permute-start | bytes 172040 | tf_op jit(solution)/shard_map/ppermute | solution.py:15
  11.3 4.7 %collective-permute-start = (f32[14,4,256]{2,1,0:T(4,128)}, f32[14,4,256]{2,1,0:T(4,128)S(1)}, u32[]{:S(2)}, u32[]{:S(2)}) collective-permute-start(f32[14,4,256]{2,1,0:T(4,128)} %get-tuple-element.12), channel_id=1, source_target_pairs={{0,4},{4,8},{8,12},{12,16},{16,20},{20,24},{24,28},{28,0},{1,5},{5... | collective-permute-start | bytes 172040 | tf_op jit(solution)/shard_map/ppermute | solution.py:15
  17.4 5.5 %collective-permute-start.5 = (f32[14,4,256]{2,1,0:T(4,128)S(1)}, f32[14,4,256]{2,1,0:T(4,128)S(1)}, u32[]{:S(2)}, u32[]{:S(2)}) collective-permute-start(f32[14,4,256]{2,1,0:T(4,128)S(1)} %bitcast.39), channel_id=1, source_target_pairs={{0,3},{1,0},{2,1},{3,2},{4,7},{5,4},{6,5},{7,6},{8,11},{9,8},{10,9... | collective-permute-start | bytes 172040 | tf_op jit(solution)/shard_map/ppermute | solution.py:15
  21.1 5.1 %collective-permute-start.4 = (f32[14,4,256]{2,1,0:T(4,128)S(1)}, f32[14,4,256]{2,1,0:T(4,128)S(1)}, u32[]{:S(2)}, u32[]{:S(2)}) collective-permute-start(f32[14,4,256]{2,1,0:T(4,128)S(1)} %bitcast.40), channel_id=1, source_target_pairs={{0,2},{1,3},{2,0},{3,1},{4,6},{5,7},{6,4},{7,5},{8,10},{9,11},{10,... | collective-permute-start | bytes 172040 | tf_op jit(solution)/shard_map/ppermute | solution.py:15
  21.2 6.0 %collective-permute-start.3 = (f32[14,4,256]{2,1,0:T(4,128)S(1)}, f32[14,4,256]{2,1,0:T(4,128)S(1)}, u32[]{:S(2)}, u32[]{:S(2)}) collective-permute-start(f32[14,4,256]{2,1,0:T(4,128)S(1)} %bitcast.41), channel_id=1, source_target_pairs={{0,1},{1,2},{2,3},{3,0},{4,5},{5,6},{6,7},{7,4},{8,9},{9,10},{10,1... | collective-permute-start | bytes 172040 | tf_op jit(solution)/shard_map/ppermute | solution.py:15

commit v4 on v3

--- a/solution.py
+++ b/solution.py
@@ -6,7 +6,7 @@
 from jax.sharding import PartitionSpec as P
 
 ROWS = 4
-PRECISION = lax.Precision.HIGHEST
+PRECISION = lax.Precision.HIGH
 
 
 def shifted(value, axis, steps):

time: 28.1 us -> 26.5 us (0.943)
  Pallas kernels: 7.39 us -> 5.77 us
    pallas_call x1, Pallas kernels: 7.39 us -> 5.77 us  [transform(): pl.pallas_call(transform_kernel, out_shape=tuple((jax.ShapeDtypeStruct((c...]
  transfers between devices with their start and end apart: 6 -> 6, of which waited for: 6 -> 6; matrix products, arithmetic and copies ran while one was open for 4% -> 5% of each run, Pallas kernels for 0% -> 0%
where the time goes in v4:
time: 26.5 us; the launch traced here: 26.3 us
  starting transfers between devices  8.67 us (33%)
  waiting for transfers between devices  8.49 us (32%)
  Pallas kernels  5.77 us (22%)
  other arithmetic  2.46 us (9%)
  matrix products  0.44 us (2%)
  local copies, waits for them, and re-layouts  0.36 us (1%)
    ppermute x6, starting transfers between devices, shifted(): return lax.ppermute(value, axis, pairs)  8.67 us
    ppermute x6, waiting for transfers between devices, shifted(): return lax.ppermute(value, axis, pairs)  8.49 us
    pallas_call x1, Pallas kernels, transform(): pl.pallas_call(transform_kernel, out_shape=tuple((jax.ShapeDtypeStruct((c...  5.77 us
    another operation x1, other arithmetic, local(): jnp.stack(routed)  0.87 us
    reduce_sum x1, other arithmetic, local(): chosen = jnp.sum(onehot[:, None, :, None] * coef[None], axis=2)  0.82 us
    broadcast_in_dim x1, other arithmetic, local(): return total[None]  0.68 us
  transfers between devices with their start and end apart: 6, of which 6 were waited for; matrix products, arithmetic and copies ran while one was open for 5% of the time, Pallas kernels for 0%

profile of v4, /device:TPU:0, one launch (start us, length us, event | category | flops | bytes accessed | tf_op | source)
XLA Modules:
  0.0 26.3 jit_solution(2583492916212587150)
XLA Ops:
  0.0 0.0 copy-start.1
  0.0 0.0 copy-start
  0.0 5.8 %shard_map.64 = (f32[14,4,256]{2,1,0:T(4,128)}, f32[14,4,256]{2,1,0:T(4,128)}, f32[14,4,256]{2,1,0:T(4,128)}, f32[14,4,256]{2,1,0:T(4,128)}, f32[4,4]{1,0:T(4,128)}) custom-call(s32[8]{0:T(128)} %dims_hbm.1, s32[4]{0:T(128)} %shift_hbm.1, f32[1,14,256,256]{3,2,1,0:T(8,128)} %env_hbm.1, f32[1,4,256,256]{3,2,1,0:T(8,128)} %mps_hbm.1), custom_call_target="tpu_custom_call" | custom-call | flops 352321536 | bytes 4947968 | tf_op jit(solution)/shard_map/pallas_call | solution.py:79
  5.8 3.4 %collective-permute-start.2 = (f32[14,4,256]{2,1,0:T(4,128)}, f32[14,4,256]{2,1,0:T(4,128)S(1)}, u32[]{:S(2)}, u32[]{:S(2)}) collective-permute-start(f32[14,4,256]{2,1,0:T(4,128)} %get-tuple-element.14), channel_id=1, source_target_pairs={{0,28},{4,0},{8,4},{12,8},{16,12},{20,16},{24,20},{28,24},{1,29},{... | collective-permute-start | bytes 172040 | tf_op jit(solution)/shard_map/ppermute | solution.py:15
  9.2 0.5 %collective-permute-start.1 = (f32[14,4,256]{2,1,0:T(4,128)}, f32[14,4,256]{2,1,0:T(4,128)S(1)}, u32[]{:S(2)}, u32[]{:S(2)}) collective-permute-start(f32[14,4,256]{2,1,0:T(4,128)} %get-tuple-element.13), channel_id=1, source_target_pairs={{0,16},{4,20},{8,24},{12,28},{16,0},{20,4},{24,8},{28,12},{1,17},{... | collective-permute-start | bytes 172040 | tf_op jit(solution)/shard_map/ppermute | solution.py:15
  9.7 0.0 collective-permute-start
  9.7 0.0 copy-done.1
  9.7 0.1 copy.16
  9.8 0.0 copy-done
  9.8 0.1 broadcast_multiply_fusion
  9.9 0.8 %multiply_reduce_fusion = f32[4,14,56]{2,1,0:T(8,128)S(1)} fusion(f32[14,4,56]{2,1,0:T(4,128)S(1)} %broadcast_multiply_fusion, f32[4,4]{1,0:T(4,128)} %get-tuple-element.10), kind=kLoop, calls=%fused_computation.5 | loop fusion | flops 21952 | bytes 25152 | tf_op jit(solution)/shard_map/reduce_sum | solution.py:113
  10.7 0.1 reshape.9
  10.9 0.4 %collective-permute-done.2 = f32[14,4,256]{2,1,0:T(4,128)S(1)} collective-permute-done((f32[14,4,256]{2,1,0:T(4,128)}, f32[14,4,256]{2,1,0:T(4,128)S(1)}, u32[]{:S(2)}, u32[]{:S(2)}) %collective-permute-start.2) | collective-permute-done | bytes 57376 | tf_op jit(solution)/shard_map/ppermute | solution.py:15
  11.3 2.2 %collective-permute-done.1 = f32[14,4,256]{2,1,0:T(4,128)S(1)} collective-permute-done((f32[14,4,256]{2,1,0:T(4,128)}, f32[14,4,256]{2,1,0:T(4,128)S(1)}, u32[]{:S(2)}, u32[]{:S(2)}) %collective-permute-start.1) | collective-permute-done | bytes 57376 | tf_op jit(solution)/shard_map/ppermute | solution.py:15
  13.6 0.8 %collective-permute-done = f32[14,4,256]{2,1,0:T(4,128)S(1)} collective-permute-done((f32[14,4,256]{2,1,0:T(4,128)}, f32[14,4,256]{2,1,0:T(4,128)S(1)}, u32[]{:S(2)}, u32[]{:S(2)}) %collective-permute-start) | collective-permute-done | bytes 57376 | tf_op jit(solution)/shard_map/ppermute | solution.py:15
  14.4 0.9 %pad_maximum_fusion = f32[4,14,4,256]{3,2,1,0:T(4,128)S(1)} fusion(f32[1,14,4,256]{3,2,1,0:T(4,128)S(1)} %bitcast.36, f32[1,14,4,256]{3,2,1,0:T(4,128)S(1)} %bitcast.37, f32[1,14,4,256]{3,2,1,0:T(4,128)S(1)} %bitcast.38, f32[1,14,4,256]{3,2,1,0:T(4,128)} %bitcast.35), kind=kLoop, calls=%fused_computation.3 | loop fusion | flops 172032 | bytes 458752 | tf_op jit(solution)/shard_map/stack | solution.py:114
  15.3 0.4 %convolution_bitcast_fusion = f32[4,14,4,256]{3,1,2,0:T(8,128)S(1)} fusion(f32[4,14,4,256]{3,2,1,0:T(4,128)S(1)} %pad_maximum_fusion, f32[4,14,4,14,1]{1,0,3,2,4:T(4,128)S(1)} %bitcast.33), kind=kOutput, calls=%fused_computation | convolution fusion | flops 38535168 | bytes 471296 | tf_op jit(solution)/shard_map/kwrc,kwv->vrc/dot_general | solution.py:114
  15.8 3.7 %collective-permute-start.5 = (f32[14,4,256]{2,1,0:T(4,128)S(1)}, f32[14,4,256]{2,1,0:T(4,128)S(1)}, u32[]{:S(2)}, u32[]{:S(2)}) collective-permute-start(f32[14,4,256]{2,1,0:T(4,128)S(1)} %bitcast.39), channel_id=1, source_target_pairs={{0,3},{1,0},{2,1},{3,2},{4,7},{5,4},{6,5},{7,6},{8,11},{9,8},{10,9... | collective-permute-start | bytes 172040 | tf_op jit(solution)/shard_map/ppermute | solution.py:15
  19.5 0.1 collective-permute-start.4
  19.6 1.0 %collective-permute-start.3 = (f32[14,4,256]{2,1,0:T(4,128)S(1)}, f32[14,4,256]{2,1,0:T(4,128)S(1)}, u32[]{:S(2)}, u32[]{:S(2)}) collective-permute-start(f32[14,4,256]{2,1,0:T(4,128)S(1)} %bitcast.41), channel_id=1, source_target_pairs={{0,1},{1,2},{2,3},{3,0},{4,5},{5,6},{6,7},{7,4},{8,9},{9,10},{10,1... | collective-permute-start | bytes 172040 | tf_op jit(solution)/shard_map/ppermute | solution.py:15
  20.7 0.6 %collective-permute-done.5 = f32[14,4,256]{2,1,0:T(4,128)S(1)} collective-permute-done((f32[14,4,256]{2,1,0:T(4,128)S(1)}, f32[14,4,256]{2,1,0:T(4,128)S(1)}, u32[]{:S(2)}, u32[]{:S(2)}) %collective-permute-start.5) | collective-permute-done | bytes 57376 | tf_op jit(solution)/shard_map/ppermute | solution.py:15
  21.3 3.4 %collective-permute-done.4 = f32[14,4,256]{2,1,0:T(4,128)S(1)} collective-permute-done((f32[14,4,256]{2,1,0:T(4,128)S(1)}, f32[14,4,256]{2,1,0:T(4,128)S(1)}, u32[]{:S(2)}, u32[]{:S(2)}) %collective-permute-start.4) | collective-permute-done | bytes 57376 | tf_op jit(solution)/shard_map/ppermute | solution.py:15
  24.6 1.0 %collective-permute-done.3 = f32[14,4,256]{2,1,0:T(4,128)S(1)} collective-permute-done((f32[14,4,256]{2,1,0:T(4,128)S(1)}, f32[14,4,256]{2,1,0:T(4,128)S(1)}, u32[]{:S(2)}, u32[]{:S(2)}) %collective-permute-start.3) | collective-permute-done | bytes 57376 | tf_op jit(solution)/shard_map/ppermute | solution.py:15
  25.6 0.7 %fusion.5 = f32[1,14,4,256]{3,2,1,0:T(4,128)} fusion(f32[14,4,256]{2,1,0:T(4,128)S(1)} %collective-permute-done.5, f32[14,4,256]{2,1,0:T(4,128)S(1)} %collective-permute-done.4, f32[14,4,256]{2,1,0:T(4,128)S(1)} %collective-permute-done.3, f32[1,14,4,256]{3,1,2,0:T(8,128)S(1)} %get-tuple-element.15), kind=kLoop, calls=%fused_computation.9 | loop fusion | flops 43008 | bytes 286720 | tf_op jit(solution)/shard_map/broadcast_in_dim | solution.py:121
  (5 shorter events, 0.2 us)
Async XLA Ops:
  0.0 9.7 %copy-start.1 = (s32[14,4]{0,1:T(4,128)S(1)}, s32[14,4]{0,1:T(4,128)}, u32[]{:S(2)}) copy-start(s32[14,4]{0,1:T(4,128)} %param.9) | copy-start | bytes 676
  0.0 9.8 %copy-start = (f32[14,4,56]{2,1,0:T(4,128)S(1)}, f32[14,4,56]{2,1,0:T(4,128)}, u32[]{:S(2)}) copy-start(f32[14,4,56]{2,1,0:T(4,128)} %param.8) | copy-start | bytes 37636
  5.8 5.5 %collective-permute-start.2 = (f32[14,4,256]{2,1,0:T(4,128)}, f32[14,4,256]{2,1,0:T(4,128)S(1)}, u32[]{:S(2)}, u32[]{:S(2)}) collective-permute-start(f32[14,4,256]{2,1,0:T(4,128)} %get-tuple-element.14), channel_id=1, source_target_pairs={{0,28},{4,0},{8,4},{12,8},{16,12},{20,16},{24,20},{28,24},{1,29},{... | collective-permute-start | bytes 172040 | tf_op jit(solution)/shard_map/ppermute | solution.py:15
  9.2 4.4 %collective-permute-start.1 = (f32[14,4,256]{2,1,0:T(4,128)}, f32[14,4,256]{2,1,0:T(4,128)S(1)}, u32[]{:S(2)}, u32[]{:S(2)}) collective-permute-start(f32[14,4,256]{2,1,0:T(4,128)} %get-tuple-element.13), channel_id=1, source_target_pairs={{0,16},{4,20},{8,24},{12,28},{16,0},{20,4},{24,8},{28,12},{1,17},{... | collective-permute-start | bytes 172040 | tf_op jit(solution)/shard_map/ppermute | solution.py:15
  9.7 4.7 %collective-permute-start = (f32[14,4,256]{2,1,0:T(4,128)}, f32[14,4,256]{2,1,0:T(4,128)S(1)}, u32[]{:S(2)}, u32[]{:S(2)}) collective-permute-start(f32[14,4,256]{2,1,0:T(4,128)} %get-tuple-element.12), channel_id=1, source_target_pairs={{0,4},{4,8},{8,12},{12,16},{16,20},{20,24},{24,28},{28,0},{1,5},{5... | collective-permute-start | bytes 172040 | tf_op jit(solution)/shard_map/ppermute | solution.py:15
  15.8 5.5 %collective-permute-start.5 = (f32[14,4,256]{2,1,0:T(4,128)S(1)}, f32[14,4,256]{2,1,0:T(4,128)S(1)}, u32[]{:S(2)}, u32[]{:S(2)}) collective-permute-start(f32[14,4,256]{2,1,0:T(4,128)S(1)} %bitcast.39), channel_id=1, source_target_pairs={{0,3},{1,0},{2,1},{3,2},{4,7},{5,4},{6,5},{7,6},{8,11},{9,8},{10,9... | collective-permute-start | bytes 172040 | tf_op jit(solution)/shard_map/ppermute | solution.py:15
  19.5 5.1 %collective-permute-start.4 = (f32[14,4,256]{2,1,0:T(4,128)S(1)}, f32[14,4,256]{2,1,0:T(4,128)S(1)}, u32[]{:S(2)}, u32[]{:S(2)}) collective-permute-start(f32[14,4,256]{2,1,0:T(4,128)S(1)} %bitcast.40), channel_id=1, source_target_pairs={{0,2},{1,3},{2,0},{3,1},{4,6},{5,7},{6,4},{7,5},{8,10},{9,11},{10,... | collective-permute-start | bytes 172040 | tf_op jit(solution)/shard_map/ppermute | solution.py:15
  19.6 6.0 %collective-permute-start.3 = (f32[14,4,256]{2,1,0:T(4,128)S(1)}, f32[14,4,256]{2,1,0:T(4,128)S(1)}, u32[]{:S(2)}, u32[]{:S(2)}) collective-permute-start(f32[14,4,256]{2,1,0:T(4,128)S(1)} %bitcast.41), channel_id=1, source_target_pairs={{0,1},{1,2},{2,3},{3,0},{4,5},{5,6},{6,7},{7,4},{8,9},{9,10},{10,1... | collective-permute-start | bytes 172040 | tf_op jit(solution)/shard_map/ppermute | solution.py:15

commit v5 on v4

--- a/solution.py
+++ b/solution.py
@@ -111,7 +111,10 @@
             routed.append(shifted(blocks[k], "sec", step))
     coef = mpo * mpo_pattern[:, :, None].astype(jnp.float32)
     chosen = jnp.sum(onehot[:, None, :, None] * coef[None], axis=2)
-    partial = jnp.einsum("kwrc,kwv->vrc", jnp.stack(routed), chosen, precision=highest)
+    partial = None
+    for k, block in enumerate(routed):
+        term = jnp.einsum("wrc,wv->vrc", block, chosen[k], precision=highest)
+        partial = term if partial is None else partial + term
     chunk = partial.shape[0] // parts
     pieces = partial.reshape((parts, chunk) + partial.shape[1:])
     total = lax.dynamic_index_in_dim(pieces, me, 0, keepdims=False)

time: 26.5 us -> 24.3 us (0.917)
  waiting for transfers between devices: 8.49 us -> 2.84 us
  starting transfers between devices: 8.67 us -> 11.2 us
  matrix products: 0.44 us -> 2.37 us
  other arithmetic: 2.46 us -> 1.56 us
    ppermute x6, waiting for transfers between devices: 8.49 us -> 2.84 us  [shifted(): return lax.ppermute(value, axis, pairs)]
    ppermute x6, starting transfers between devices: 8.67 us -> 11.2 us  [shifted(): return lax.ppermute(value, axis, pairs)]
    dot_general x1 -> x4, matrix products: 0.44 us -> 2.37 us  [local(): term = jnp.einsum('wrc,wv->vrc', block, chosen[k], precision=highest)]
    another operation x1 -> x0, other arithmetic: 0.87 us -> none  [local(): jnp.stack(routed)]
  transfers between devices with their start and end apart: 6 -> 6, of which waited for: 6 -> 3; matrix products, arithmetic and copies ran while one was open for 5% -> 12% of each run, Pallas kernels for 0% -> 0%
where the time goes in v5:
time: 24.3 us; the launch traced here: 24.1 us
  starting transfers between devices  11.2 us (46%)
  Pallas kernels  5.77 us (24%)
  waiting for transfers between devices  2.84 us (12%)
  matrix products  2.37 us (10%)
  other arithmetic  1.56 us (6%)
    ppermute x6, starting transfers between devices, shifted(): return lax.ppermute(value, axis, pairs)  11.2 us
    pallas_call x1, Pallas kernels, transform(): pl.pallas_call(transform_kernel, out_shape=tuple((jax.ShapeDtypeStruct((c...  5.77 us
    ppermute x6, waiting for transfers between devices, shifted(): return lax.ppermute(value, axis, pairs)  2.84 us
    dot_general x4, matrix products, local(): term = jnp.einsum('wrc,wv->vrc', block, chosen[k], precision=highest)  2.37 us
    reduce_sum x1, other arithmetic, local(): chosen = jnp.sum(onehot[:, None, :, None] * coef[None], axis=2)  0.82 us
    broadcast_in_dim x1, other arithmetic, local(): return total[None]  0.66 us
  transfers between devices with their start and end apart: 6, of which 3 were waited for; matrix products, arithmetic and copies ran while one was open for 12% of the time, Pallas kernels for 0%

profile of v5, /device:TPU:0, one launch (start us, length us, event | category | flops | bytes accessed | tf_op | source)
XLA Modules:
  0.0 24.1 jit_solution(15740477404378728550)
XLA Ops:
  0.0 0.0 copy-start.1
  0.0 0.0 copy-start
  0.0 5.8 %shard_map.64 = (f32[14,4,256]{2,1,0:T(4,128)}, f32[14,4,256]{2,1,0:T(4,128)}, f32[14,4,256]{2,1,0:T(4,128)}, f32[14,4,256]{2,1,0:T(4,128)}, f32[4,4]{1,0:T(4,128)}) custom-call(s32[8]{0:T(128)} %dims_hbm.1, s32[4]{0:T(128)} %shift_hbm.1, f32[1,14,256,256]{3,2,1,0:T(8,128)} %env_hbm.1, f32[1,4,256,256]{3,2,1,0:T(8,128)} %mps_hbm.1), custom_call_target="tpu_custom_call" | custom-call | flops 352321536 | bytes 4947968 | tf_op jit(solution)/shard_map/pallas_call | solution.py:79
  5.8 0.5 %collective-permute-start = (f32[14,4,256]{2,1,0:T(4,128)}, f32[14,4,256]{2,1,0:T(4,128)S(1)}, u32[]{:S(2)}, u32[]{:S(2)}) collective-permute-start(f32[14,4,256]{2,1,0:T(4,128)} %get-tuple-element.12), channel_id=1, source_target_pairs={{0,4},{4,8},{8,12},{12,16},{16,20},{20,24},{24,28},{28,0},{1,5},{5... | collective-permute-start | bytes 172040 | tf_op jit(solution)/shard_map/ppermute | solution.py:15
  6.3 2.9 %collective-permute-start.2 = (f32[14,4,256]{2,1,0:T(4,128)}, f32[14,4,256]{2,1,0:T(4,128)S(1)}, u32[]{:S(2)}, u32[]{:S(2)}) collective-permute-start(f32[14,4,256]{2,1,0:T(4,128)} %get-tuple-element.14), channel_id=1, source_target_pairs={{0,28},{4,0},{8,4},{12,8},{16,12},{20,16},{24,20},{28,24},{1,29},{... | collective-permute-start | bytes 172040 | tf_op jit(solution)/shard_map/ppermute | solution.py:15
  9.2 2.2 %collective-permute-start.1 = (f32[14,4,256]{2,1,0:T(4,128)}, f32[14,4,256]{2,1,0:T(4,128)S(1)}, u32[]{:S(2)}, u32[]{:S(2)}) collective-permute-start(f32[14,4,256]{2,1,0:T(4,128)} %get-tuple-element.13), channel_id=1, source_target_pairs={{0,16},{4,20},{8,24},{12,28},{16,0},{20,4},{24,8},{28,12},{1,17},{... | collective-permute-start | bytes 172040 | tf_op jit(solution)/shard_map/ppermute | solution.py:15
  11.4 0.0 copy-done.1
  11.4 0.1 copy.22
  11.5 0.0 copy-done
  11.6 0.1 broadcast_multiply_fusion
  11.6 0.8 %multiply_reduce_fusion = f32[4,14,56]{2,1,0:T(8,128)S(1)} fusion(f32[14,4,56]{2,1,0:T(4,128)S(1)} %broadcast_multiply_fusion, f32[4,4]{1,0:T(4,128)} %get-tuple-element.10), kind=kLoop, calls=%fused_computation.3 | loop fusion | flops 21952 | bytes 25152 | tf_op jit(solution)/shard_map/reduce_sum | solution.py:113
  12.5 1.2 %fusion.5 = f32[56,4,256]{2,0,1:T(8,128)S(1)} fusion(f32[14,4,256]{2,1,0:T(4,128)} %get-tuple-element.11, f32[4,14,56]{2,1,0:T(8,128)S(1)} %multiply_reduce_fusion), kind=kOutput, calls=%fused_computation.8 | convolution fusion | flops 9633792 | bytes 294912 | tf_op jit(solution)/shard_map/wrc,wv->vrc/dot_general | solution.py:116
  13.7 0.0 collective-permute-done
  13.7 0.4 %convolution_add_fusion.1 = f32[56,4,256]{2,0,1:T(8,128)S(1)} fusion(f32[56,4,256]{2,0,1:T(8,128)S(1)} %fusion.5, f32[14,4,256]{2,1,0:T(4,128)S(1)} %collective-permute-done, f32[4,14,56]{2,1,0:T(8,128)S(1)} %multiply_reduce_fusion), kind=kOutput, calls=%fused_computation.2 | convolution fusion | flops 9691136 | bytes 524288 | tf_op jit(solution)/shard_map/wrc,wv->vrc/dot_general | solution.py:116
  14.1 0.0 collective-permute-done.2
  14.1 0.4 %fusion.1 = f32[56,4,256]{2,0,1:T(8,128)S(1)} fusion(f32[14,4,256]{2,1,0:T(4,128)S(1)} %collective-permute-done.2, f32[4,14,56]{2,1,0:T(8,128)S(1)} %multiply_reduce_fusion), kind=kOutput, calls=%fused_computation.4 | convolution fusion | flops 9633792 | bytes 294912 | tf_op jit(solution)/shard_map/wrc,wv->vrc/dot_general | solution.py:116
  14.5 0.0 collective-permute-done.1
  14.5 0.4 %fusion = f32[56,4,256]{2,0,1:T(8,128)S(1)} fusion(f32[56,4,256]{2,0,1:T(8,128)S(1)} %fusion.1, f32[56,4,256]{2,0,1:T(8,128)S(1)} %convolution_add_fusion.1, f32[14,4,256]{2,1,0:T(4,128)S(1)} %collective-permute-done.1, f32[4,14,56]{2,1,0:T(8,128)S(1)} %multiply_reduce_fusion), kind=kOutput, calls=%fused_computation.1 | convolution fusion | flops 9748480 | bytes 753664 | tf_op jit(solution)/shard_map/wrc,wv->vrc/dot_general | solution.py:116
  14.9 0.1 copy.27
  15.1 1.6 %collective-permute-start.3 = (f32[14,4,256]{2,1,0:T(4,128)S(1)}, f32[14,4,256]{2,1,0:T(4,128)S(1)}, u32[]{:S(2)}, u32[]{:S(2)}) collective-permute-start(f32[14,4,256]{2,1,0:T(4,128)S(1)} %get-tuple-element.15), channel_id=1, source_target_pairs={{0,1},{1,2},{2,3},{3,0},{4,5},{5,6},{6,7},{7,4},{8,9},{9,10},{10,1... | collective-permute-start | bytes 172040 | tf_op jit(solution)/shard_map/ppermute | solution.py:15
  16.7 2.6 %collective-permute-start.4 = (f32[14,4,256]{2,1,0:T(4,128)S(1)}, f32[14,4,256]{2,1,0:T(4,128)S(1)}, u32[]{:S(2)}, u32[]{:S(2)}) collective-permute-start(f32[14,4,256]{2,1,0:T(4,128)S(1)} %get-tuple-element.17), channel_id=1, source_target_pairs={{0,2},{1,3},{2,0},{3,1},{4,6},{5,7},{6,4},{7,5},{8,10},{9,11},{10,... | collective-permute-start | bytes 172040 | tf_op jit(solution)/shard_map/ppermute | solution.py:15
  19.3 1.3 %collective-permute-start.5 = (f32[14,4,256]{2,1,0:T(4,128)S(1)}, f32[14,4,256]{2,1,0:T(4,128)S(1)}, u32[]{:S(2)}, u32[]{:S(2)}) collective-permute-start(f32[14,4,256]{2,1,0:T(4,128)S(1)} %get-tuple-element.16), channel_id=1, source_target_pairs={{0,3},{1,0},{2,1},{3,2},{4,7},{5,4},{6,5},{7,6},{8,11},{9,8},{10,9... | collective-permute-start | bytes 172040 | tf_op jit(solution)/shard_map/ppermute | solution.py:15
  20.6 0.8 %collective-permute-done.3 = f32[14,4,256]{2,1,0:T(4,128)S(1)} collective-permute-done((f32[14,4,256]{2,1,0:T(4,128)S(1)}, f32[14,4,256]{2,1,0:T(4,128)S(1)}, u32[]{:S(2)}, u32[]{:S(2)}) %collective-permute-start.3) | collective-permute-done | bytes 57376 | tf_op jit(solution)/shard_map/ppermute | solution.py:15
  21.5 0.6 %collective-permute-done.4 = f32[14,4,256]{2,1,0:T(4,128)S(1)} collective-permute-done((f32[14,4,256]{2,1,0:T(4,128)S(1)}, f32[14,4,256]{2,1,0:T(4,128)S(1)}, u32[]{:S(2)}, u32[]{:S(2)}) %collective-permute-start.4) | collective-permute-done | bytes 57376 | tf_op jit(solution)/shard_map/ppermute | solution.py:15
  22.1 1.4 %collective-permute-done.5 = f32[14,4,256]{2,1,0:T(4,128)S(1)} collective-permute-done((f32[14,4,256]{2,1,0:T(4,128)S(1)}, f32[14,4,256]{2,1,0:T(4,128)S(1)}, u32[]{:S(2)}, u32[]{:S(2)}) %collective-permute-start.5) | collective-permute-done | bytes 57376 | tf_op jit(solution)/shard_map/ppermute | solution.py:15
  23.5 0.7 %fusion.9 = f32[1,14,4,256]{3,2,1,0:T(4,128)} fusion(f32[14,4,256]{2,1,0:T(4,128)S(1)} %collective-permute-done.5, f32[14,4,256]{2,1,0:T(4,128)S(1)} %collective-permute-done.4, f32[14,4,256]{2,1,0:T(4,128)S(1)} %collective-permute-done.3, f32[4,14,4,256]{3,2,1,0:T(4,128)S(1)} %bitcast.34, s32[]{:T(128)S(6)} %select_n.28), kind=kLoop, calls=%fused_computation.13 | loop fusion | flops 43008 | bytes 286724 | tf_op jit(solution)/shard_map/broadcast_in_dim | solution.py:124
  (2 shorter events, 0.0 us)
Async XLA Ops:
  0.0 11.4 %copy-start.1 = (s32[14,4]{0,1:T(4,128)S(1)}, s32[14,4]{0,1:T(4,128)}, u32[]{:S(2)}) copy-start(s32[14,4]{0,1:T(4,128)} %param.9) | copy-start | bytes 676
  0.0 11.5 %copy-start = (f32[14,4,56]{2,1,0:T(4,128)S(1)}, f32[14,4,56]{2,1,0:T(4,128)}, u32[]{:S(2)}) copy-start(f32[14,4,56]{2,1,0:T(4,128)} %param.8) | copy-start | bytes 37636
  5.8 7.9 %collective-permute-start = (f32[14,4,256]{2,1,0:T(4,128)}, f32[14,4,256]{2,1,0:T(4,128)S(1)}, u32[]{:S(2)}, u32[]{:S(2)}) collective-permute-start(f32[14,4,256]{2,1,0:T(4,128)} %get-tuple-element.12), channel_id=1, source_target_pairs={{0,4},{4,8},{8,12},{12,16},{16,20},{20,24},{24,28},{28,0},{1,5},{5... | collective-permute-start | bytes 172040 | tf_op jit(solution)/shard_map/ppermute | solution.py:15
  6.3 7.8 %collective-permute-start.2 = (f32[14,4,256]{2,1,0:T(4,128)}, f32[14,4,256]{2,1,0:T(4,128)S(1)}, u32[]{:S(2)}, u32[]{:S(2)}) collective-permute-start(f32[14,4,256]{2,1,0:T(4,128)} %get-tuple-element.14), channel_id=1, source_target_pairs={{0,28},{4,0},{8,4},{12,8},{16,12},{20,16},{24,20},{28,24},{1,29},{... | collective-permute-start | bytes 172040 | tf_op jit(solution)/shard_map/ppermute | solution.py:15
  9.2 5.3 %collective-permute-start.1 = (f32[14,4,256]{2,1,0:T(4,128)}, f32[14,4,256]{2,1,0:T(4,128)S(1)}, u32[]{:S(2)}, u32[]{:S(2)}) collective-permute-start(f32[14,4,256]{2,1,0:T(4,128)} %get-tuple-element.13), channel_id=1, source_target_pairs={{0,16},{4,20},{8,24},{12,28},{16,0},{20,4},{24,8},{28,12},{1,17},{... | collective-permute-start | bytes 172040 | tf_op jit(solution)/shard_map/ppermute | solution.py:15
  15.1 6.4 %collective-permute-start.3 = (f32[14,4,256]{2,1,0:T(4,128)S(1)}, f32[14,4,256]{2,1,0:T(4,128)S(1)}, u32[]{:S(2)}, u32[]{:S(2)}) collective-permute-start(f32[14,4,256]{2,1,0:T(4,128)S(1)} %get-tuple-element.15), channel_id=1, source_target_pairs={{0,1},{1,2},{2,3},{3,0},{4,5},{5,6},{6,7},{7,4},{8,9},{9,10},{10,1... | collective-permute-start | bytes 172040 | tf_op jit(solution)/shard_map/ppermute | solution.py:15
  16.7 5.4 %collective-permute-start.4 = (f32[14,4,256]{2,1,0:T(4,128)S(1)}, f32[14,4,256]{2,1,0:T(4,128)S(1)}, u32[]{:S(2)}, u32[]{:S(2)}) collective-permute-start(f32[14,4,256]{2,1,0:T(4,128)S(1)} %get-tuple-element.17), channel_id=1, source_target_pairs={{0,2},{1,3},{2,0},{3,1},{4,6},{5,7},{6,4},{7,5},{8,10},{9,11},{10,... | collective-permute-start | bytes 172040 | tf_op jit(solution)/shard_map/ppermute | solution.py:15
  19.3 4.2 %collective-permute-start.5 = (f32[14,4,256]{2,1,0:T(4,128)S(1)}, f32[14,4,256]{2,1,0:T(4,128)S(1)}, u32[]{:S(2)}, u32[]{:S(2)}) collective-permute-start(f32[14,4,256]{2,1,0:T(4,128)S(1)} %get-tuple-element.16), channel_id=1, source_target_pairs={{0,3},{1,0},{2,1},{3,2},{4,7},{5,4},{6,5},{7,6},{8,11},{9,8},{10,9... | collective-permute-start | bytes 172040 | tf_op jit(solution)/shard_map/ppermute | solution.py:15

commit v6 on v5

--- a/solution.py
+++ b/solution.py
@@ -17,6 +17,16 @@
 
 def sector_steps(sectors):
     return (0, 1, sectors // 2, sectors - 1)
+
+
+def split_dot(left_parts, right):
+    both, left_hi = left_parts
+    rows = left_hi.shape[0]
+    right_hi = right.astype(jnp.bfloat16)
+    right_lo = (right - right_hi.astype(jnp.float32)).astype(jnp.bfloat16)
+    first = jnp.dot(both, right_hi, preferred_element_type=jnp.float32)
+    second = jnp.dot(left_hi, right_lo, preferred_element_type=jnp.float32)
+    return first[:rows] + first[rows:] + second
 
 
 def transform_kernel(dims_hbm, shift_hbm, env_hbm, mps_hbm, *refs):
@@ -57,10 +67,12 @@
         left_sc[k * ROWS:(k + 1) * ROWS, :] = jnp.transpose(masked[:, :128])[:ROWS]
         onehot_ref[k:k + 1, :] = (lanes == pick).astype(jnp.float32)
     left = left_sc[...]
+    left_hi = left.astype(jnp.bfloat16)
+    left_lo = (left - left_hi.astype(jnp.float32)).astype(jnp.bfloat16)
+    left_parts = (jnp.concatenate([left_hi, left_lo], axis=0), left_hi)
     for j in range(channels):
         loads[j].wait()
-        half = jnp.dot(left, env_sc[j], precision=PRECISION,
-                       preferred_element_type=jnp.float32)
+        half = split_dot(left_parts, env_sc[j])
         for k in range(states):
             half_sc[k, j * ROWS:(j + 1) * ROWS, :] = half[k * ROWS:(k + 1) * ROWS]
     for k in range(states):

time: 24.3 us -> 23.8 us (0.979)
  Pallas kernels: 5.77 us -> 5.2 us
    pallas_call x1, Pallas kernels: 5.77 us -> 5.2 us  [transform(): pl.pallas_call(transform_kernel, out_shape=tuple((jax.ShapeDtypeStruct((c...]
  transfers between devices with their start and end apart: 6 -> 6, of which waited for: 3 -> 3; matrix products, arithmetic and copies ran while one was open for 12% -> 13% of each run, Pallas kernels for 0% -> 0%
where the time goes in v6:
time: 23.8 us; the launch traced here: 23.6 us
  starting transfers between devices  11.2 us (47%)
  Pallas kernels  5.2 us (22%)
  waiting for transfers between devices  2.84 us (12%)
  matrix products  2.37 us (10%)
  other arithmetic  1.56 us (7%)
    ppermute x6, starting transfers between devices, shifted(): return lax.ppermute(value, axis, pairs)  11.2 us
    pallas_call x1, Pallas kernels, transform(): pl.pallas_call(transform_kernel, out_shape=tuple((jax.ShapeDtypeStruct((c...  5.2 us
    ppermute x6, waiting for transfers between devices, shifted(): return lax.ppermute(value, axis, pairs)  2.84 us
    dot_general x4, matrix products, local(): term = jnp.einsum('wrc,wv->vrc', block, chosen[k], precision=highest)  2.37 us
    reduce_sum x1, other arithmetic, local(): chosen = jnp.sum(onehot[:, None, :, None] * coef[None], axis=2)  0.82 us
    broadcast_in_dim x1, other arithmetic, local(): return total[None]  0.66 us
  transfers between devices with their start and end apart: 6, of which 3 were waited for; matrix products, arithmetic and copies ran while one was open for 13% of the time, Pallas kernels for 0%

profile of v6, /device:TPU:0, one launch (start us, length us, event | category | flops | bytes accessed | tf_op | source)
XLA Modules:
  0.0 23.6 jit_solution(17597640152051223387)
XLA Ops:
  0.0 0.0 copy-start.1
  0.0 0.0 copy-start
  0.0 5.2 %shard_map.64 = (f32[14,4,256]{2,1,0:T(4,128)}, f32[14,4,256]{2,1,0:T(4,128)}, f32[14,4,256]{2,1,0:T(4,128)}, f32[14,4,256]{2,1,0:T(4,128)}, f32[4,4]{1,0:T(4,128)}) custom-call(s32[8]{0:T(128)} %dims_hbm.1, s32[4]{0:T(128)} %shift_hbm.1, f32[1,14,256,256]{3,2,1,0:T(8,128)} %env_hbm.1, f32[1,4,256,256]{3,2,1,0:T(8,128)} %mps_hbm.1), custom_call_target="tpu_custom_call" | custom-call | flops 352321536 | bytes 4947968 | tf_op jit(solution)/shard_map/pallas_call | solution.py:91
  5.2 0.5 %collective-permute-start = (f32[14,4,256]{2,1,0:T(4,128)}, f32[14,4,256]{2,1,0:T(4,128)S(1)}, u32[]{:S(2)}, u32[]{:S(2)}) collective-permute-start(f32[14,4,256]{2,1,0:T(4,128)} %get-tuple-element.12), channel_id=1, source_target_pairs={{0,4},{4,8},{8,12},{12,16},{16,20},{20,24},{24,28},{28,0},{1,5},{5... | collective-permute-start | bytes 172040 | tf_op jit(solution)/shard_map/ppermute | solution.py:15
  5.7 2.9 %collective-permute-start.2 = (f32[14,4,256]{2,1,0:T(4,128)}, f32[14,4,256]{2,1,0:T(4,128)S(1)}, u32[]{:S(2)}, u32[]{:S(2)}) collective-permute-start(f32[14,4,256]{2,1,0:T(4,128)} %get-tuple-element.14), channel_id=1, source_target_pairs={{0,28},{4,0},{8,4},{12,8},{16,12},{20,16},{24,20},{28,24},{1,29},{... | collective-permute-start | bytes 172040 | tf_op jit(solution)/shard_map/ppermute | solution.py:15
  8.7 2.2 %collective-permute-start.1 = (f32[14,4,256]{2,1,0:T(4,128)}, f32[14,4,256]{2,1,0:T(4,128)S(1)}, u32[]{:S(2)}, u32[]{:S(2)}) collective-permute-start(f32[14,4,256]{2,1,0:T(4,128)} %get-tuple-element.13), channel_id=1, source_target_pairs={{0,16},{4,20},{8,24},{12,28},{16,0},{20,4},{24,8},{28,12},{1,17},{... | collective-permute-start | bytes 172040 | tf_op jit(solution)/shard_map/ppermute | solution.py:15
  10.9 0.0 copy-done.1
  10.9 0.1 copy.22
  11.0 0.0 copy-done
  11.0 0.1 broadcast_multiply_fusion
  11.1 0.8 %multiply_reduce_fusion = f32[4,14,56]{2,1,0:T(8,128)S(1)} fusion(f32[14,4,56]{2,1,0:T(4,128)S(1)} %broadcast_multiply_fusion, f32[4,4]{1,0:T(4,128)} %get-tuple-element.10), kind=kLoop, calls=%fused_computation.3 | loop fusion | flops 21952 | bytes 25152 | tf_op jit(solution)/shard_map/reduce_sum | solution.py:125
  11.9 1.2 %fusion.5 = f32[56,4,256]{2,0,1:T(8,128)S(1)} fusion(f32[14,4,256]{2,1,0:T(4,128)} %get-tuple-element.11, f32[4,14,56]{2,1,0:T(8,128)S(1)} %multiply_reduce_fusion), kind=kOutput, calls=%fused_computation.8 | convolution fusion | flops 9633792 | bytes 294912 | tf_op jit(solution)/shard_map/wrc,wv->vrc/dot_general | solution.py:128
  13.2 0.0 collective-permute-done
  13.2 0.4 %convolution_add_fusion.1 = f32[56,4,256]{2,0,1:T(8,128)S(1)} fusion(f32[56,4,256]{2,0,1:T(8,128)S(1)} %fusion.5, f32[14,4,256]{2,1,0:T(4,128)S(1)} %collective-permute-done, f32[4,14,56]{2,1,0:T(8,128)S(1)} %multiply_reduce_fusion), kind=kOutput, calls=%fused_computation.2 | convolution fusion | flops 9691136 | bytes 524288 | tf_op jit(solution)/shard_map/wrc,wv->vrc/dot_general | solution.py:128
  13.6 0.0 collective-permute-done.2
  13.6 0.4 %fusion.1 = f32[56,4,256]{2,0,1:T(8,128)S(1)} fusion(f32[14,4,256]{2,1,0:T(4,128)S(1)} %collective-permute-done.2, f32[4,14,56]{2,1,0:T(8,128)S(1)} %multiply_reduce_fusion), kind=kOutput, calls=%fused_computation.4 | convolution fusion | flops 9633792 | bytes 294912 | tf_op jit(solution)/shard_map/wrc,wv->vrc/dot_general | solution.py:128
  14.0 0.0 collective-permute-done.1
  14.0 0.4 %fusion = f32[56,4,256]{2,0,1:T(8,128)S(1)} fusion(f32[56,4,256]{2,0,1:T(8,128)S(1)} %fusion.1, f32[56,4,256]{2,0,1:T(8,128)S(1)} %convolution_add_fusion.1, f32[14,4,256]{2,1,0:T(4,128)S(1)} %collective-permute-done.1, f32[4,14,56]{2,1,0:T(8,128)S(1)} %multiply_reduce_fusion), kind=kOutput, calls=%fused_computation.1 | convolution fusion | flops 9748480 | bytes 753664 | tf_op jit(solution)/shard_map/wrc,wv->vrc/dot_general | solution.py:128
  14.4 0.1 copy.27
  14.5 1.6 %collective-permute-start.3 = (f32[14,4,256]{2,1,0:T(4,128)S(1)}, f32[14,4,256]{2,1,0:T(4,128)S(1)}, u32[]{:S(2)}, u32[]{:S(2)}) collective-permute-start(f32[14,4,256]{2,1,0:T(4,128)S(1)} %get-tuple-element.15), channel_id=1, source_target_pairs={{0,1},{1,2},{2,3},{3,0},{4,5},{5,6},{6,7},{7,4},{8,9},{9,10},{10,1... | collective-permute-start | bytes 172040 | tf_op jit(solution)/shard_map/ppermute | solution.py:15
  16.1 2.6 %collective-permute-start.4 = (f32[14,4,256]{2,1,0:T(4,128)S(1)}, f32[14,4,256]{2,1,0:T(4,128)S(1)}, u32[]{:S(2)}, u32[]{:S(2)}) collective-permute-start(f32[14,4,256]{2,1,0:T(4,128)S(1)} %get-tuple-element.17), channel_id=1, source_target_pairs={{0,2},{1,3},{2,0},{3,1},{4,6},{5,7},{6,4},{7,5},{8,10},{9,11},{10,... | collective-permute-start | bytes 172040 | tf_op jit(solution)/shard_map/ppermute | solution.py:15
  18.7 1.3 %collective-permute-start.5 = (f32[14,4,256]{2,1,0:T(4,128)S(1)}, f32[14,4,256]{2,1,0:T(4,128)S(1)}, u32[]{:S(2)}, u32[]{:S(2)}) collective-permute-start(f32[14,4,256]{2,1,0:T(4,128)S(1)} %get-tuple-element.16), channel_id=1, source_target_pairs={{0,3},{1,0},{2,1},{3,2},{4,7},{5,4},{6,5},{7,6},{8,11},{9,8},{10,9... | collective-permute-start | bytes 172040 | tf_op jit(solution)/shard_map/ppermute | solution.py:15
  20.1 0.8 %collective-permute-done.3 = f32[14,4,256]{2,1,0:T(4,128)S(1)} collective-permute-done((f32[14,4,256]{2,1,0:T(4,128)S(1)}, f32[14,4,256]{2,1,0:T(4,128)S(1)}, u32[]{:S(2)}, u32[]{:S(2)}) %collective-permute-start.3) | collective-permute-done | bytes 57376 | tf_op jit(solution)/shard_map/ppermute | solution.py:15
  20.9 0.6 %collective-permute-done.4 = f32[14,4,256]{2,1,0:T(4,128)S(1)} collective-permute-done((f32[14,4,256]{2,1,0:T(4,128)S(1)}, f32[14,4,256]{2,1,0:T(4,128)S(1)}, u32[]{:S(2)}, u32[]{:S(2)}) %collective-permute-start.4) | collective-permute-done | bytes 57376 | tf_op jit(solution)/shard_map/ppermute | solution.py:15
  21.5 1.4 %collective-permute-done.5 = f32[14,4,256]{2,1,0:T(4,128)S(1)} collective-permute-done((f32[14,4,256]{2,1,0:T(4,128)S(1)}, f32[14,4,256]{2,1,0:T(4,128)S(1)}, u32[]{:S(2)}, u32[]{:S(2)}) %collective-permute-start.5) | collective-permute-done | bytes 57376 | tf_op jit(solution)/shard_map/ppermute | solution.py:15
  22.9 0.7 %fusion.9 = f32[1,14,4,256]{3,2,1,0:T(4,128)} fusion(f32[14,4,256]{2,1,0:T(4,128)S(1)} %collective-permute-done.5, f32[14,4,256]{2,1,0:T(4,128)S(1)} %collective-permute-done.4, f32[14,4,256]{2,1,0:T(4,128)S(1)} %collective-permute-done.3, f32[4,14,4,256]{3,2,1,0:T(4,128)S(1)} %bitcast.34, s32[]{:T(128)S(6)} %select_n.28), kind=kLoop, calls=%fused_computation.13 | loop fusion | flops 43008 | bytes 286724 | tf_op jit(solution)/shard_map/broadcast_in_dim | solution.py:136
  (2 shorter events, 0.0 us)
Async XLA Ops:
  0.0 10.9 %copy-start.1 = (s32[14,4]{0,1:T(4,128)S(1)}, s32[14,4]{0,1:T(4,128)}, u32[]{:S(2)}) copy-start(s32[14,4]{0,1:T(4,128)} %param.9) | copy-start | bytes 676
  0.0 11.0 %copy-start = (f32[14,4,56]{2,1,0:T(4,128)S(1)}, f32[14,4,56]{2,1,0:T(4,128)}, u32[]{:S(2)}) copy-start(f32[14,4,56]{2,1,0:T(4,128)} %param.8) | copy-start | bytes 37636
  5.2 7.9 %collective-permute-start = (f32[14,4,256]{2,1,0:T(4,128)}, f32[14,4,256]{2,1,0:T(4,128)S(1)}, u32[]{:S(2)}, u32[]{:S(2)}) collective-permute-start(f32[14,4,256]{2,1,0:T(4,128)} %get-tuple-element.12), channel_id=1, source_target_pairs={{0,4},{4,8},{8,12},{12,16},{16,20},{20,24},{24,28},{28,0},{1,5},{5... | collective-permute-start | bytes 172040 | tf_op jit(solution)/shard_map/ppermute | solution.py:15
  5.7 7.8 %collective-permute-start.2 = (f32[14,4,256]{2,1,0:T(4,128)}, f32[14,4,256]{2,1,0:T(4,128)S(1)}, u32[]{:S(2)}, u32[]{:S(2)}) collective-permute-start(f32[14,4,256]{2,1,0:T(4,128)} %get-tuple-element.14), channel_id=1, source_target_pairs={{0,28},{4,0},{8,4},{12,8},{16,12},{20,16},{24,20},{28,24},{1,29},{... | collective-permute-start | bytes 172040 | tf_op jit(solution)/shard_map/ppermute | solution.py:15
  8.7 5.3 %collective-permute-start.1 = (f32[14,4,256]{2,1,0:T(4,128)}, f32[14,4,256]{2,1,0:T(4,128)S(1)}, u32[]{:S(2)}, u32[]{:S(2)}) collective-permute-start(f32[14,4,256]{2,1,0:T(4,128)} %get-tuple-element.13), channel_id=1, source_target_pairs={{0,16},{4,20},{8,24},{12,28},{16,0},{20,4},{24,8},{28,12},{1,17},{... | collective-permute-start | bytes 172040 | tf_op jit(solution)/shard_map/ppermute | solution.py:15
  14.5 6.4 %collective-permute-start.3 = (f32[14,4,256]{2,1,0:T(4,128)S(1)}, f32[14,4,256]{2,1,0:T(4,128)S(1)}, u32[]{:S(2)}, u32[]{:S(2)}) collective-permute-start(f32[14,4,256]{2,1,0:T(4,128)S(1)} %get-tuple-element.15), channel_id=1, source_target_pairs={{0,1},{1,2},{2,3},{3,0},{4,5},{5,6},{6,7},{7,4},{8,9},{9,10},{10,1... | collective-permute-start | bytes 172040 | tf_op jit(solution)/shard_map/ppermute | solution.py:15
  16.1 5.4 %collective-permute-start.4 = (f32[14,4,256]{2,1,0:T(4,128)S(1)}, f32[14,4,256]{2,1,0:T(4,128)S(1)}, u32[]{:S(2)}, u32[]{:S(2)}) collective-permute-start(f32[14,4,256]{2,1,0:T(4,128)S(1)} %get-tuple-element.17), channel_id=1, source_target_pairs={{0,2},{1,3},{2,0},{3,1},{4,6},{5,7},{6,4},{7,5},{8,10},{9,11},{10,... | collective-permute-start | bytes 172040 | tf_op jit(solution)/shard_map/ppermute | solution.py:15
  18.7 4.2 %collective-permute-start.5 = (f32[14,4,256]{2,1,0:T(4,128)S(1)}, f32[14,4,256]{2,1,0:T(4,128)S(1)}, u32[]{:S(2)}, u32[]{:S(2)}) collective-permute-start(f32[14,4,256]{2,1,0:T(4,128)S(1)} %get-tuple-element.16), channel_id=1, source_target_pairs={{0,3},{1,0},{2,1},{3,2},{4,7},{5,4},{6,5},{7,6},{8,11},{9,8},{10,9... | collective-permute-start | bytes 172040 | tf_op jit(solution)/shard_map/ppermute | solution.py:15

commit v7 on v6

--- a/solution.py
+++ b/solution.py
@@ -125,7 +125,7 @@
     chosen = jnp.sum(onehot[:, None, :, None] * coef[None], axis=2)
     partial = None
     for k, block in enumerate(routed):
-        term = jnp.einsum("wrc,wv->vrc", block, chosen[k], precision=highest)
+        term = jnp.einsum("wrc,wv->vrc", block, chosen[k], precision=lax.Precision.HIGH)
         partial = term if partial is None else partial + term
     chunk = partial.shape[0] // parts
     pieces = partial.reshape((parts, chunk) + partial.shape[1:])

time: 23.8 us -> 23.4 us (0.983)
  matrix products: 2.37 us -> 1.99 us
    dot_general x4, matrix products: 2.37 us -> 1.99 us  [local(): jnp.einsum('wrc,wv->vrc', block, chosen[k], precision=lax.Precision.HIGH)]
  transfers between devices with their start and end apart: 6 -> 6, of which waited for: 3 -> 3; matrix products, arithmetic and copies ran while one was open for 13% -> 12% of each run, Pallas kernels for 0% -> 0%
where the time goes in v7:
time: 23.4 us; the launch traced here: 23.2 us
  starting transfers between devices  11.3 us (48%)
  Pallas kernels  5.2 us (22%)
  waiting for transfers between devices  2.83 us (12%)
  matrix products  1.99 us (9%)
  other arithmetic  1.56 us (7%)
    ppermute x6, starting transfers between devices, shifted(): return lax.ppermute(value, axis, pairs)  11.3 us
    pallas_call x1, Pallas kernels, transform(): pl.pallas_call(transform_kernel, out_shape=tuple((jax.ShapeDtypeStruct((c...  5.2 us
    ppermute x6, waiting for transfers between devices, shifted(): return lax.ppermute(value, axis, pairs)  2.83 us
    dot_general x4, matrix products, local(): jnp.einsum('wrc,wv->vrc', block, chosen[k], precision=lax.Precision.HIGH)  1.99 us
    reduce_sum x1, other arithmetic, local(): chosen = jnp.sum(onehot[:, None, :, None] * coef[None], axis=2)  0.82 us
    broadcast_in_dim x1, other arithmetic, local(): return total[None]  0.66 us
  transfers between devices with their start and end apart: 6, of which 3 were waited for; matrix products, arithmetic and copies ran while one was open for 12% of the time, Pallas kernels for 0%

profile of v7, /device:TPU:0, one launch (start us, length us, event | category | flops | bytes accessed | tf_op | source)
XLA Modules:
  0.0 23.2 jit_solution(5638506733054818517)
XLA Ops:
  0.0 0.0 copy-start.1
  0.0 0.0 copy-start
  0.0 5.2 %shard_map.64 = (f32[14,4,256]{2,1,0:T(4,128)}, f32[14,4,256]{2,1,0:T(4,128)}, f32[14,4,256]{2,1,0:T(4,128)}, f32[14,4,256]{2,1,0:T(4,128)}, f32[4,4]{1,0:T(4,128)}) custom-call(s32[8]{0:T(128)} %dims_hbm.1, s32[4]{0:T(128)} %shift_hbm.1, f32[1,14,256,256]{3,2,1,0:T(8,128)} %env_hbm.1, f32[1,4,256,256]{3,2,1,0:T(8,128)} %mps_hbm.1), custom_call_target="tpu_custom_call" | custom-call | flops 352321536 | bytes 4947968 | tf_op jit(solution)/shard_map/pallas_call | solution.py:91
  5.2 0.5 %collective-permute-start = (f32[14,4,256]{2,1,0:T(4,128)}, f32[14,4,256]{2,1,0:T(4,128)S(1)}, u32[]{:S(2)}, u32[]{:S(2)}) collective-permute-start(f32[14,4,256]{2,1,0:T(4,128)} %get-tuple-element.12), channel_id=1, source_target_pairs={{0,4},{4,8},{8,12},{12,16},{16,20},{20,24},{24,28},{28,0},{1,5},{5... | collective-permute-start | bytes 172040 | tf_op jit(solution)/shard_map/ppermute | solution.py:15
  5.7 2.9 %collective-permute-start.2 = (f32[14,4,256]{2,1,0:T(4,128)}, f32[14,4,256]{2,1,0:T(4,128)S(1)}, u32[]{:S(2)}, u32[]{:S(2)}) collective-permute-start(f32[14,4,256]{2,1,0:T(4,128)} %get-tuple-element.14), channel_id=1, source_target_pairs={{0,28},{4,0},{8,4},{12,8},{16,12},{20,16},{24,20},{28,24},{1,29},{... | collective-permute-start | bytes 172040 | tf_op jit(solution)/shard_map/ppermute | solution.py:15
  8.7 2.2 %collective-permute-start.1 = (f32[14,4,256]{2,1,0:T(4,128)}, f32[14,4,256]{2,1,0:T(4,128)S(1)}, u32[]{:S(2)}, u32[]{:S(2)}) collective-permute-start(f32[14,4,256]{2,1,0:T(4,128)} %get-tuple-element.13), channel_id=1, source_target_pairs={{0,16},{4,20},{8,24},{12,28},{16,0},{20,4},{24,8},{28,12},{1,17},{... | collective-permute-start | bytes 172040 | tf_op jit(solution)/shard_map/ppermute | solution.py:15
  10.9 0.0 copy-done.1
  10.9 0.1 copy.22
  11.0 0.0 copy-done
  11.0 0.1 broadcast_multiply_fusion
  11.1 0.8 %multiply_reduce_fusion = f32[4,14,56]{2,1,0:T(8,128)S(1)} fusion(f32[14,4,56]{2,1,0:T(4,128)S(1)} %broadcast_multiply_fusion, f32[4,4]{1,0:T(4,128)} %get-tuple-element.10), kind=kLoop, calls=%fused_computation.3 | loop fusion | flops 21952 | bytes 25152 | tf_op jit(solution)/shard_map/reduce_sum | solution.py:125
  11.9 1.1 %fusion.5 = f32[56,4,256]{2,0,1:T(8,128)S(1)} fusion(f32[14,4,256]{2,1,0:T(4,128)} %get-tuple-element.11, f32[4,14,56]{2,1,0:T(8,128)S(1)} %multiply_reduce_fusion), kind=kOutput, calls=%fused_computation.8 | convolution fusion | flops 4816896 | bytes 294912 | tf_op jit(solution)/shard_map/wrc,wv->vrc/dot_general | solution.py:128
  13.1 0.0 collective-permute-done
  13.1 0.3 %convolution_add_fusion.1 = f32[56,4,256]{2,0,1:T(8,128)S(1)} fusion(f32[56,4,256]{2,0,1:T(8,128)S(1)} %fusion.5, f32[14,4,256]{2,1,0:T(4,128)S(1)} %collective-permute-done, f32[4,14,56]{2,1,0:T(8,128)S(1)} %multiply_reduce_fusion), kind=kOutput, calls=%fused_computation.2 | convolution fusion | flops 4874240 | bytes 524288 | tf_op jit(solution)/shard_map/wrc,wv->vrc/dot_general | solution.py:128
  13.4 0.0 collective-permute-done.2
  13.4 0.3 %fusion.1 = f32[56,4,256]{2,0,1:T(8,128)S(1)} fusion(f32[14,4,256]{2,1,0:T(4,128)S(1)} %collective-permute-done.2, f32[4,14,56]{2,1,0:T(8,128)S(1)} %multiply_reduce_fusion), kind=kOutput, calls=%fused_computation.4 | convolution fusion | flops 4816896 | bytes 294912 | tf_op jit(solution)/shard_map/wrc,wv->vrc/dot_general | solution.py:128
  13.7 0.0 collective-permute-done.1
  13.7 0.3 %fusion = f32[56,4,256]{2,0,1:T(8,128)S(1)} fusion(f32[56,4,256]{2,0,1:T(8,128)S(1)} %fusion.1, f32[56,4,256]{2,0,1:T(8,128)S(1)} %convolution_add_fusion.1, f32[14,4,256]{2,1,0:T(4,128)S(1)} %collective-permute-done.1, f32[4,14,56]{2,1,0:T(8,128)S(1)} %multiply_reduce_fusion), kind=kOutput, calls=%fused_computation.1 | convolution fusion | flops 4931584 | bytes 753664 | tf_op jit(solution)/shard_map/wrc,wv->vrc/dot_general | solution.py:128
  14.0 0.1 copy.27
  14.1 1.7 %collective-permute-start.3 = (f32[14,4,256]{2,1,0:T(4,128)S(1)}, f32[14,4,256]{2,1,0:T(4,128)S(1)}, u32[]{:S(2)}, u32[]{:S(2)}) collective-permute-start(f32[14,4,256]{2,1,0:T(4,128)S(1)} %get-tuple-element.15), channel_id=1, source_target_pairs={{0,1},{1,2},{2,3},{3,0},{4,5},{5,6},{6,7},{7,4},{8,9},{9,10},{10,1... | collective-permute-start | bytes 172040 | tf_op jit(solution)/shard_map/ppermute | solution.py:15
  15.8 2.6 %collective-permute-start.4 = (f32[14,4,256]{2,1,0:T(4,128)S(1)}, f32[14,4,256]{2,1,0:T(4,128)S(1)}, u32[]{:S(2)}, u32[]{:S(2)}) collective-permute-start(f32[14,4,256]{2,1,0:T(4,128)S(1)} %get-tuple-element.17), channel_id=1, source_target_pairs={{0,2},{1,3},{2,0},{3,1},{4,6},{5,7},{6,4},{7,5},{8,10},{9,11},{10,... | collective-permute-start | bytes 172040 | tf_op jit(solution)/shard_map/ppermute | solution.py:15
  18.4 1.4 %collective-permute-start.5 = (f32[14,4,256]{2,1,0:T(4,128)S(1)}, f32[14,4,256]{2,1,0:T(4,128)S(1)}, u32[]{:S(2)}, u32[]{:S(2)}) collective-permute-start(f32[14,4,256]{2,1,0:T(4,128)S(1)} %get-tuple-element.16), channel_id=1, source_target_pairs={{0,3},{1,0},{2,1},{3,2},{4,7},{5,4},{6,5},{7,6},{8,11},{9,8},{10,9... | collective-permute-start | bytes 172040 | tf_op jit(solution)/shard_map/ppermute | solution.py:15
  19.7 0.8 %collective-permute-done.3 = f32[14,4,256]{2,1,0:T(4,128)S(1)} collective-permute-done((f32[14,4,256]{2,1,0:T(4,128)S(1)}, f32[14,4,256]{2,1,0:T(4,128)S(1)}, u32[]{:S(2)}, u32[]{:S(2)}) %collective-permute-start.3) | collective-permute-done | bytes 57376 | tf_op jit(solution)/shard_map/ppermute | solution.py:15
  20.6 0.6 %collective-permute-done.4 = f32[14,4,256]{2,1,0:T(4,128)S(1)} collective-permute-done((f32[14,4,256]{2,1,0:T(4,128)S(1)}, f32[14,4,256]{2,1,0:T(4,128)S(1)}, u32[]{:S(2)}, u32[]{:S(2)}) %collective-permute-start.4) | collective-permute-done | bytes 57376 | tf_op jit(solution)/shard_map/ppermute | solution.py:15
  21.2 1.4 %collective-permute-done.5 = f32[14,4,256]{2,1,0:T(4,128)S(1)} collective-permute-done((f32[14,4,256]{2,1,0:T(4,128)S(1)}, f32[14,4,256]{2,1,0:T(4,128)S(1)}, u32[]{:S(2)}, u32[]{:S(2)}) %collective-permute-start.5) | collective-permute-done | bytes 57376 | tf_op jit(solution)/shard_map/ppermute | solution.py:15
  22.6 0.7 %fusion.9 = f32[1,14,4,256]{3,2,1,0:T(4,128)} fusion(f32[14,4,256]{2,1,0:T(4,128)S(1)} %collective-permute-done.5, f32[14,4,256]{2,1,0:T(4,128)S(1)} %collective-permute-done.4, f32[14,4,256]{2,1,0:T(4,128)S(1)} %collective-permute-done.3, f32[4,14,4,256]{3,2,1,0:T(4,128)S(1)} %bitcast.34, s32[]{:T(128)S(6)} %select_n.28), kind=kLoop, calls=%fused_computation.13 | loop fusion | flops 43008 | bytes 286724 | tf_op jit(solution)/shard_map/broadcast_in_dim | solution.py:136
  (2 shorter events, 0.0 us)
Async XLA Ops:
  0.0 10.9 %copy-start.1 = (s32[14,4]{0,1:T(4,128)S(1)}, s32[14,4]{0,1:T(4,128)}, u32[]{:S(2)}) copy-start(s32[14,4]{0,1:T(4,128)} %param.9) | copy-start | bytes 676
  0.0 11.0 %copy-start = (f32[14,4,56]{2,1,0:T(4,128)S(1)}, f32[14,4,56]{2,1,0:T(4,128)}, u32[]{:S(2)}) copy-start(f32[14,4,56]{2,1,0:T(4,128)} %param.8) | copy-start | bytes 37636
  5.2 7.8 %collective-permute-start = (f32[14,4,256]{2,1,0:T(4,128)}, f32[14,4,256]{2,1,0:T(4,128)S(1)}, u32[]{:S(2)}, u32[]{:S(2)}) collective-permute-start(f32[14,4,256]{2,1,0:T(4,128)} %get-tuple-element.12), channel_id=1, source_target_pairs={{0,4},{4,8},{8,12},{12,16},{16,20},{20,24},{24,28},{28,0},{1,5},{5... | collective-permute-start | bytes 172040 | tf_op jit(solution)/shard_map/ppermute | solution.py:15
  5.7 7.7 %collective-permute-start.2 = (f32[14,4,256]{2,1,0:T(4,128)}, f32[14,4,256]{2,1,0:T(4,128)S(1)}, u32[]{:S(2)}, u32[]{:S(2)}) collective-permute-start(f32[14,4,256]{2,1,0:T(4,128)} %get-tuple-element.14), channel_id=1, source_target_pairs={{0,28},{4,0},{8,4},{12,8},{16,12},{20,16},{24,20},{28,24},{1,29},{... | collective-permute-start | bytes 172040 | tf_op jit(solution)/shard_map/ppermute | solution.py:15
  8.7 5.0 %collective-permute-start.1 = (f32[14,4,256]{2,1,0:T(4,128)}, f32[14,4,256]{2,1,0:T(4,128)S(1)}, u32[]{:S(2)}, u32[]{:S(2)}) collective-permute-start(f32[14,4,256]{2,1,0:T(4,128)} %get-tuple-element.13), channel_id=1, source_target_pairs={{0,16},{4,20},{8,24},{12,28},{16,0},{20,4},{24,8},{28,12},{1,17},{... | collective-permute-start | bytes 172040 | tf_op jit(solution)/shard_map/ppermute | solution.py:15
  14.1 6.5 %collective-permute-start.3 = (f32[14,4,256]{2,1,0:T(4,128)S(1)}, f32[14,4,256]{2,1,0:T(4,128)S(1)}, u32[]{:S(2)}, u32[]{:S(2)}) collective-permute-start(f32[14,4,256]{2,1,0:T(4,128)S(1)} %get-tuple-element.15), channel_id=1, source_target_pairs={{0,1},{1,2},{2,3},{3,0},{4,5},{5,6},{6,7},{7,4},{8,9},{9,10},{10,1... | collective-permute-start | bytes 172040 | tf_op jit(solution)/shard_map/ppermute | solution.py:15
  15.8 5.4 %collective-permute-start.4 = (f32[14,4,256]{2,1,0:T(4,128)S(1)}, f32[14,4,256]{2,1,0:T(4,128)S(1)}, u32[]{:S(2)}, u32[]{:S(2)}) collective-permute-start(f32[14,4,256]{2,1,0:T(4,128)S(1)} %get-tuple-element.17), channel_id=1, source_target_pairs={{0,2},{1,3},{2,0},{3,1},{4,6},{5,7},{6,4},{7,5},{8,10},{9,11},{10,... | collective-permute-start | bytes 172040 | tf_op jit(solution)/shard_map/ppermute | solution.py:15
  18.4 4.2 %collective-permute-start.5 = (f32[14,4,256]{2,1,0:T(4,128)S(1)}, f32[14,4,256]{2,1,0:T(4,128)S(1)}, u32[]{:S(2)}, u32[]{:S(2)}) collective-permute-start(f32[14,4,256]{2,1,0:T(4,128)S(1)} %get-tuple-element.16), channel_id=1, source_target_pairs={{0,3},{1,0},{2,1},{3,2},{4,7},{5,4},{6,5},{7,6},{8,11},{9,8},{10,9... | collective-permute-start | bytes 172040 | tf_op jit(solution)/shard_map/ppermute | solution.py:15

commit v8 on v7

v8 whole, which is shorter than its diff:
```python
import jax
import jax.numpy as jnp
from jax import lax
from jax.experimental import pallas as pl
from jax.experimental.pallas import tpu as pltpu
from jax.sharding import PartitionSpec as P

ROWS = 4
PRECISION = lax.Precision.HIGH
GRID = 2


def shifted(value, axis, steps):
    count = lax.axis_size(axis)
    pairs = [(source, (source + steps) % count) for source in range(count)]
    return lax.ppermute(value, axis, pairs)


def sector_steps(sectors):
    return (0, 1, sectors // 2, sectors - 1)


def split_dot(left_parts, right):
    both, left_hi = left_parts
    rows = left_hi.shape[0]
    right_hi = right.astype(jnp.bfloat16)
    right_lo = (right - right_hi.astype(jnp.float32)).astype(jnp.bfloat16)
    first = jnp.dot(both, right_hi, preferred_element_type=jnp.float32)
    second = jnp.dot(left_hi, right_lo, preferred_element_type=jnp.float32)
    return first[:rows] + first[rows:] + second


def transform_kernel(dims_hbm, shift_hbm, env_ref, mps_ref, *refs):
    count = len(refs) - 7
    blocks_refs = refs[:count]
    onehot_ref, dims_sc, shift_sc, masked_sc, left_sc, half_sc, sems = refs[count:]
    sectors = dims_sc.shape[0]
    states = mps_ref.shape[1]
    block_channels = env_ref.shape[1]
    steps_total = pl.num_programs(0)
    width = mps_ref.shape[-1]
    here = lax.axis_index("sec")
    step = pl.program_id(0)

    @pl.when(step == 0)
    def _():
        small = [
            pltpu.make_async_copy(dims_hbm, dims_sc, sems.at[0]),
            pltpu.make_async_copy(shift_hbm, shift_sc, sems.at[1]),
        ]
        for copy in small:
            copy.start()
        for copy in small:
            copy.wait()
        dims_in = dims_sc[here]
        rows = lax.broadcasted_iota(jnp.int32, (width, width), 0)
        cols = lax.broadcasted_iota(jnp.int32, (width, width), 1)
        lanes = lax.broadcasted_iota(jnp.int32, (1, states), 1)
        for k, shift in enumerate(sector_steps(sectors)):
            pick = 0
            for s in range(states):
                pick = pick + jnp.where(lax.rem(shift_sc[s], sectors) == shift, s, 0)
            dims_out = dims_sc[lax.rem(here + shift, sectors)]
            live = (rows < dims_in) & (cols < dims_out)
            masked = jnp.where(live, mps_ref[0, pick], 0.0)
            masked_sc[k] = masked
            left_sc[k * ROWS:(k + 1) * ROWS, :] = jnp.transpose(masked[:, :128])[:ROWS]
            onehot_ref[k:k + 1, :] = (lanes == pick).astype(jnp.float32)

    left = left_sc[...]
    left_hi = left.astype(jnp.bfloat16)
    left_lo = (left - left_hi.astype(jnp.float32)).astype(jnp.bfloat16)
    left_parts = (jnp.concatenate([left_hi, left_lo], axis=0), left_hi)
    for block_index in range(half_sc.shape[1] // ROWS // block_channels):
        @pl.when(step == block_index)
        def _():
            for jj in range(block_channels):
                j = block_index * block_channels + jj
                half = split_dot(left_parts, env_ref[0, jj])
                for k in range(states):
                    half_sc[k, j * ROWS:(j + 1) * ROWS, :] = half[k * ROWS:(k + 1) * ROWS]

    @pl.when(step == steps_total - 1)
    def _():
        channels = half_sc.shape[1] // ROWS
        for k in range(states):
            full = jnp.dot(half_sc[k], masked_sc[k], precision=PRECISION,
                           preferred_element_type=jnp.float32)
            for j in range(channels):
                blocks_refs[k][j] = full[j * ROWS:(j + 1) * ROWS]


def transform(sector_dims, state_shift, environment, mps):
    channels, width = environment.shape[1], environment.shape[-1]
    states = mps.shape[1]
    grid = GRID if channels % GRID == 0 else 1
    block_channels = channels // grid
    anywhere = pl.BlockSpec(memory_space=pl.ANY)
    whole = lambda shape: pl.BlockSpec(shape, lambda i: (0,) * len(shape))
    flops = 2 * states * ROWS * width * width * channels * 2
    return pl.pallas_call(
        transform_kernel,
        grid=(grid,),
        out_shape=tuple(
            jax.ShapeDtypeStruct((channels, ROWS, width), jnp.float32) for _ in range(states)
        ) + (jax.ShapeDtypeStruct((states, states), jnp.float32),),
        in_specs=[
            anywhere, anywhere,
            pl.BlockSpec((1, block_channels, width, width), lambda i: (0, i, 0, 0)),
            whole((1, states, width, width)),
        ],
        out_specs=tuple(whole((channels, ROWS, width)) for _ in range(states))
        + (whole((states, states)),),
        scratch_shapes=[
            pltpu.SMEM(sector_dims.shape, jnp.int32),
            pltpu.SMEM(state_shift.shape, jnp.int32),
            pltpu.VMEM((states, width, width), jnp.float32),
            pltpu.VMEM((states * ROWS, width), jnp.float32),
            pltpu.VMEM((states, channels * ROWS, width), jnp.float32),
            pltpu.SemaphoreType.DMA((2,)),
        ],
        cost_estimate=pl.CostEstimate(
            flops=6 * flops, transcendentals=0,
            bytes_accessed=4 * (environment.size + mps.size + states * channels * ROWS * width)),
    )(sector_dims, state_shift, environment, mps)


def local(environment, mps, mpo, mpo_pattern, state_shift, sector_dims):
    highest = lax.Precision.HIGHEST
    sectors = lax.axis_size("sec")
    parts = lax.axis_size("op")
    me = lax.axis_index("op")
    *blocks, onehot = transform(sector_dims, state_shift, environment, mps)
    routed = [blocks[0]]
    for k, step in enumerate(sector_steps(sectors)):
        if k:
            routed.append(shifted(blocks[k], "sec", step))
    coef = mpo * mpo_pattern[:, :, None].astype(jnp.float32)
    chosen = jnp.sum(onehot[:, None, :, None] * coef[None], axis=2)
    partial = None
    for k, block in enumerate(routed):
        term = jnp.einsum("wrc,wv->vrc", block, chosen[k], precision=lax.Precision.HIGH)
        partial = term if partial is None else partial + term
    chunk = partial.shape[0] // parts
    pieces = partial.reshape((parts, chunk) + partial.shape[1:])
    total = lax.dynamic_index_in_dim(pieces, me, 0, keepdims=False)
    for step in range(1, parts):
        send = lax.dynamic_index_in_dim(pieces, (me + step) % parts, 0, keepdims=False)
        total = total + shifted(send, "op", step)
    return total[None]


def solution(mesh):
    in_specs = (
        P("sec", "op", None, None),
        P("sec", None, None, None),
        P("op", None, None),
        P("op", None),
        P(),
        P(),
    )
    out_specs = P("sec", "op", None, None)
    return jax.shard_map(local, mesh=mesh, in_specs=in_specs, out_specs=out_specs, check_vma=False)
```

time: 23.4 us -> 22.9 us (0.979)
  Pallas kernels: 5.2 us -> 4.64 us
    pallas_call x1, Pallas kernels: 5.2 us -> 4.64 us  [transform(): pl.pallas_call(transform_kernel, grid=(grid,), out_shape=tuple((jax.Shape...]
where the time goes in v8:
time: 22.9 us; the launch traced here: 22.7 us
  starting transfers between devices  11.3 us (49%)
  Pallas kernels  4.64 us (20%)
  waiting for transfers between devices  2.84 us (12%)
  matrix products  1.99 us (9%)
  other arithmetic  1.56 us (7%)
    ppermute x6, starting transfers between devices, shifted(): return lax.ppermute(value, axis, pairs)  11.3 us
    pallas_call x1, Pallas kernels, transform(): pl.pallas_call(transform_kernel, grid=(grid,), out_shape=tuple((jax.Shape...  4.64 us
    ppermute x6, waiting for transfers between devices, shifted(): return lax.ppermute(value, axis, pairs)  2.84 us
    dot_general x4, matrix products, local(): jnp.einsum('wrc,wv->vrc', block, chosen[k], precision=lax.Precision.HIGH)  1.99 us
    reduce_sum x1, other arithmetic, local(): chosen = jnp.sum(onehot[:, None, :, None] * coef[None], axis=2)  0.82 us
    broadcast_in_dim x1, other arithmetic, local(): return total[None]  0.66 us
  transfers between devices with their start and end apart: 6, of which 3 were waited for; matrix products, arithmetic and copies ran while one was open for 12% of the time, Pallas kernels for 0%

profile of v8, /device:TPU:0, one launch (start us, length us, event | category | flops | bytes accessed | tf_op | source)
XLA Modules:
  0.0 22.7 jit_solution(5233065497457894882)
XLA Ops:
  0.0 0.0 copy-start.1
  0.0 0.0 copy-start
  0.0 4.6 %shard_map.64 = (f32[14,4,256]{2,1,0:T(4,128)}, f32[14,4,256]{2,1,0:T(4,128)}, f32[14,4,256]{2,1,0:T(4,128)}, f32[14,4,256]{2,1,0:T(4,128)}, f32[4,4]{1,0:T(4,128)}) custom-call(s32[8]{0:T(128)} %dims_hbm.1, s32[4]{0:T(128)} %shift_hbm.1, f32[1,14,256,256]{3,2,1,0:T(8,128)} %env_ref.1, f32[1,4,256,256]{3,2,1,0:T(8,128)} %mps_ref.1), custom_call_target="tpu_custom_call" | custom-call | flops 352321536 | bytes 4947968 | tf_op jit(solution)/shard_map/pallas_call | solution.py:101
  4.7 0.5 %collective-permute-start = (f32[14,4,256]{2,1,0:T(4,128)}, f32[14,4,256]{2,1,0:T(4,128)S(1)}, u32[]{:S(2)}, u32[]{:S(2)}) collective-permute-start(f32[14,4,256]{2,1,0:T(4,128)} %get-tuple-element.12), channel_id=1, source_target_pairs={{0,4},{4,8},{8,12},{12,16},{16,20},{20,24},{24,28},{28,0},{1,5},{5... | collective-permute-start | bytes 172040 | tf_op jit(solution)/shard_map/ppermute | solution.py:16
  5.2 2.9 %collective-permute-start.2 = (f32[14,4,256]{2,1,0:T(4,128)}, f32[14,4,256]{2,1,0:T(4,128)S(1)}, u32[]{:S(2)}, u32[]{:S(2)}) collective-permute-start(f32[14,4,256]{2,1,0:T(4,128)} %get-tuple-element.14), channel_id=1, source_target_pairs={{0,28},{4,0},{8,4},{12,8},{16,12},{20,16},{24,20},{28,24},{1,29},{... | collective-permute-start | bytes 172040 | tf_op jit(solution)/shard_map/ppermute | solution.py:16
  8.1 2.2 %collective-permute-start.1 = (f32[14,4,256]{2,1,0:T(4,128)}, f32[14,4,256]{2,1,0:T(4,128)S(1)}, u32[]{:S(2)}, u32[]{:S(2)}) collective-permute-start(f32[14,4,256]{2,1,0:T(4,128)} %get-tuple-element.13), channel_id=1, source_target_pairs={{0,16},{4,20},{8,24},{12,28},{16,0},{20,4},{24,8},{28,12},{1,17},{... | collective-permute-start | bytes 172040 | tf_op jit(solution)/shard_map/ppermute | solution.py:16
  10.3 0.0 copy-done.1
  10.3 0.1 copy.22
  10.4 0.0 copy-done
  10.4 0.1 broadcast_multiply_fusion
  10.5 0.8 %multiply_reduce_fusion = f32[4,14,56]{2,1,0:T(8,128)S(1)} fusion(f32[14,4,56]{2,1,0:T(4,128)S(1)} %broadcast_multiply_fusion, f32[4,4]{1,0:T(4,128)} %get-tuple-element.10), kind=kLoop, calls=%fused_computation.3 | loop fusion | flops 21952 | bytes 25152 | tf_op jit(solution)/shard_map/reduce_sum | solution.py:139
  11.3 1.1 %fusion.5 = f32[56,4,256]{2,0,1:T(8,128)S(1)} fusion(f32[14,4,256]{2,1,0:T(4,128)} %get-tuple-element.11, f32[4,14,56]{2,1,0:T(8,128)S(1)} %multiply_reduce_fusion), kind=kOutput, calls=%fused_computation.8 | convolution fusion | flops 4816896 | bytes 294912 | tf_op jit(solution)/shard_map/wrc,wv->vrc/dot_general | solution.py:142
  12.5 0.0 collective-permute-done
  12.5 0.3 %convolution_add_fusion.1 = f32[56,4,256]{2,0,1:T(8,128)S(1)} fusion(f32[56,4,256]{2,0,1:T(8,128)S(1)} %fusion.5, f32[14,4,256]{2,1,0:T(4,128)S(1)} %collective-permute-done, f32[4,14,56]{2,1,0:T(8,128)S(1)} %multiply_reduce_fusion), kind=kOutput, calls=%fused_computation.2 | convolution fusion | flops 4874240 | bytes 524288 | tf_op jit(solution)/shard_map/wrc,wv->vrc/dot_general | solution.py:142
  12.8 0.0 collective-permute-done.2
  12.8 0.3 %fusion.1 = f32[56,4,256]{2,0,1:T(8,128)S(1)} fusion(f32[14,4,256]{2,1,0:T(4,128)S(1)} %collective-permute-done.2, f32[4,14,56]{2,1,0:T(8,128)S(1)} %multiply_reduce_fusion), kind=kOutput, calls=%fused_computation.4 | convolution fusion | flops 4816896 | bytes 294912 | tf_op jit(solution)/shard_map/wrc,wv->vrc/dot_general | solution.py:142
  13.1 0.0 collective-permute-done.1
  13.1 0.3 %fusion = f32[56,4,256]{2,0,1:T(8,128)S(1)} fusion(f32[56,4,256]{2,0,1:T(8,128)S(1)} %fusion.1, f32[56,4,256]{2,0,1:T(8,128)S(1)} %convolution_add_fusion.1, f32[14,4,256]{2,1,0:T(4,128)S(1)} %collective-permute-done.1, f32[4,14,56]{2,1,0:T(8,128)S(1)} %multiply_reduce_fusion), kind=kOutput, calls=%fused_computation.1 | convolution fusion | flops 4931584 | bytes 753664 | tf_op jit(solution)/shard_map/wrc,wv->vrc/dot_general | solution.py:142
  13.4 0.1 copy.27
  13.6 1.7 %collective-permute-start.3 = (f32[14,4,256]{2,1,0:T(4,128)S(1)}, f32[14,4,256]{2,1,0:T(4,128)S(1)}, u32[]{:S(2)}, u32[]{:S(2)}) collective-permute-start(f32[14,4,256]{2,1,0:T(4,128)S(1)} %get-tuple-element.15), channel_id=1, source_target_pairs={{0,1},{1,2},{2,3},{3,0},{4,5},{5,6},{6,7},{7,4},{8,9},{9,10},{10,1... | collective-permute-start | bytes 172040 | tf_op jit(solution)/shard_map/ppermute | solution.py:16
  15.2 2.6 %collective-permute-start.4 = (f32[14,4,256]{2,1,0:T(4,128)S(1)}, f32[14,4,256]{2,1,0:T(4,128)S(1)}, u32[]{:S(2)}, u32[]{:S(2)}) collective-permute-start(f32[14,4,256]{2,1,0:T(4,128)S(1)} %get-tuple-element.17), channel_id=1, source_target_pairs={{0,2},{1,3},{2,0},{3,1},{4,6},{5,7},{6,4},{7,5},{8,10},{9,11},{10,... | collective-permute-start | bytes 172040 | tf_op jit(solution)/shard_map/ppermute | solution.py:16
  17.8 1.3 %collective-permute-start.5 = (f32[14,4,256]{2,1,0:T(4,128)S(1)}, f32[14,4,256]{2,1,0:T(4,128)S(1)}, u32[]{:S(2)}, u32[]{:S(2)}) collective-permute-start(f32[14,4,256]{2,1,0:T(4,128)S(1)} %get-tuple-element.16), channel_id=1, source_target_pairs={{0,3},{1,0},{2,1},{3,2},{4,7},{5,4},{6,5},{7,6},{8,11},{9,8},{10,9... | collective-permute-start | bytes 172040 | tf_op jit(solution)/shard_map/ppermute | solution.py:16
  19.2 0.8 %collective-permute-done.3 = f32[14,4,256]{2,1,0:T(4,128)S(1)} collective-permute-done((f32[14,4,256]{2,1,0:T(4,128)S(1)}, f32[14,4,256]{2,1,0:T(4,128)S(1)}, u32[]{:S(2)}, u32[]{:S(2)}) %collective-permute-start.3) | collective-permute-done | bytes 57376 | tf_op jit(solution)/shard_map/ppermute | solution.py:16
  20.0 0.6 %collective-permute-done.4 = f32[14,4,256]{2,1,0:T(4,128)S(1)} collective-permute-done((f32[14,4,256]{2,1,0:T(4,128)S(1)}, f32[14,4,256]{2,1,0:T(4,128)S(1)}, u32[]{:S(2)}, u32[]{:S(2)}) %collective-permute-start.4) | collective-permute-done | bytes 57376 | tf_op jit(solution)/shard_map/ppermute | solution.py:16
  20.6 1.4 %collective-permute-done.5 = f32[14,4,256]{2,1,0:T(4,128)S(1)} collective-permute-done((f32[14,4,256]{2,1,0:T(4,128)S(1)}, f32[14,4,256]{2,1,0:T(4,128)S(1)}, u32[]{:S(2)}, u32[]{:S(2)}) %collective-permute-start.5) | collective-permute-done | bytes 57376 | tf_op jit(solution)/shard_map/ppermute | solution.py:16
  22.0 0.7 %fusion.9 = f32[1,14,4,256]{3,2,1,0:T(4,128)} fusion(f32[14,4,256]{2,1,0:T(4,128)S(1)} %collective-permute-done.5, f32[14,4,256]{2,1,0:T(4,128)S(1)} %collective-permute-done.4, f32[14,4,256]{2,1,0:T(4,128)S(1)} %collective-permute-done.3, f32[4,14,4,256]{3,2,1,0:T(4,128)S(1)} %bitcast.34, s32[]{:T(128)S(6)} %select_n.28), kind=kLoop, calls=%fused_computation.13 | loop fusion | flops 43008 | bytes 286724 | tf_op jit(solution)/shard_map/broadcast_in_dim | solution.py:150
  (2 shorter events, 0.0 us)
Async XLA Ops:
  0.0 10.3 %copy-start.1 = (s32[14,4]{0,1:T(4,128)S(1)}, s32[14,4]{0,1:T(4,128)}, u32[]{:S(2)}) copy-start(s32[14,4]{0,1:T(4,128)} %param.9) | copy-start | bytes 676
  0.0 10.4 %copy-start = (f32[14,4,56]{2,1,0:T(4,128)S(1)}, f32[14,4,56]{2,1,0:T(4,128)}, u32[]{:S(2)}) copy-start(f32[14,4,56]{2,1,0:T(4,128)} %param.8) | copy-start | bytes 37636
  4.7 7.9 %collective-permute-start = (f32[14,4,256]{2,1,0:T(4,128)}, f32[14,4,256]{2,1,0:T(4,128)S(1)}, u32[]{:S(2)}, u32[]{:S(2)}) collective-permute-start(f32[14,4,256]{2,1,0:T(4,128)} %get-tuple-element.12), channel_id=1, source_target_pairs={{0,4},{4,8},{8,12},{12,16},{16,20},{20,24},{24,28},{28,0},{1,5},{5... | collective-permute-start | bytes 172040 | tf_op jit(solution)/shard_map/ppermute | solution.py:16
  5.2 7.7 %collective-permute-start.2 = (f32[14,4,256]{2,1,0:T(4,128)}, f32[14,4,256]{2,1,0:T(4,128)S(1)}, u32[]{:S(2)}, u32[]{:S(2)}) collective-permute-start(f32[14,4,256]{2,1,0:T(4,128)} %get-tuple-element.14), channel_id=1, source_target_pairs={{0,28},{4,0},{8,4},{12,8},{16,12},{20,16},{24,20},{28,24},{1,29},{... | collective-permute-start | bytes 172040 | tf_op jit(solution)/shard_map/ppermute | solution.py:16
  8.1 5.0 %collective-permute-start.1 = (f32[14,4,256]{2,1,0:T(4,128)}, f32[14,4,256]{2,1,0:T(4,128)S(1)}, u32[]{:S(2)}, u32[]{:S(2)}) collective-permute-start(f32[14,4,256]{2,1,0:T(4,128)} %get-tuple-element.13), channel_id=1, source_target_pairs={{0,16},{4,20},{8,24},{12,28},{16,0},{20,4},{24,8},{28,12},{1,17},{... | collective-permute-start | bytes 172040 | tf_op jit(solution)/shard_map/ppermute | solution.py:16
  13.6 6.5 %collective-permute-start.3 = (f32[14,4,256]{2,1,0:T(4,128)S(1)}, f32[14,4,256]{2,1,0:T(4,128)S(1)}, u32[]{:S(2)}, u32[]{:S(2)}) collective-permute-start(f32[14,4,256]{2,1,0:T(4,128)S(1)} %get-tuple-element.15), channel_id=1, source_target_pairs={{0,1},{1,2},{2,3},{3,0},{4,5},{5,6},{6,7},{7,4},{8,9},{9,10},{10,1... | collective-permute-start | bytes 172040 | tf_op jit(solution)/shard_map/ppermute | solution.py:16
  15.2 5.4 %collective-permute-start.4 = (f32[14,4,256]{2,1,0:T(4,128)S(1)}, f32[14,4,256]{2,1,0:T(4,128)S(1)}, u32[]{:S(2)}, u32[]{:S(2)}) collective-permute-start(f32[14,4,256]{2,1,0:T(4,128)S(1)} %get-tuple-element.17), channel_id=1, source_target_pairs={{0,2},{1,3},{2,0},{3,1},{4,6},{5,7},{6,4},{7,5},{8,10},{9,11},{10,... | collective-permute-start | bytes 172040 | tf_op jit(solution)/shard_map/ppermute | solution.py:16
  17.8 4.2 %collective-permute-start.5 = (f32[14,4,256]{2,1,0:T(4,128)S(1)}, f32[14,4,256]{2,1,0:T(4,128)S(1)}, u32[]{:S(2)}, u32[]{:S(2)}) collective-permute-start(f32[14,4,256]{2,1,0:T(4,128)S(1)} %get-tuple-element.16), channel_id=1, source_target_pairs={{0,3},{1,0},{2,1},{3,2},{4,7},{5,4},{6,5},{7,6},{8,11},{9,8},{10,9... | collective-permute-start | bytes 172040 | tf_op jit(solution)/shard_map/ppermute | solution.py:16
